TPU v7x, 32 devices: a whole 2x2x4 slice. The times are simulated.
32 devices in a mesh: fsdp: 4 (over z), tp: 8 (over y, x, core).
Axes of the slice: x: 2, y: 2, z: 4, core: 2. Of those that a mesh axis runs over, the one named last changes fastest.
Arguments:
- tokens: bfloat16 [8192, 2048], P(('fsdp', 'tp')), may hold values from -6 to 6
- seq_len: int32 [8], replicated, may hold values from 256 to 1792, as said below
- seq_group: int32 [8], replicated, may hold values from 0 to 3, as said below
- ln1_gain: float32 [2048], replicated, may hold values from 0.1 to 1.9
- ln1_bias: float32 [2048], replicated, may hold values from -1.75 to 1.75
- qkv_weight: bfloat16 [2048, 3, 2048], P('fsdp', None, 'tp'), may hold values from -0.125 to 0.125
- qv_bias: float32 [2, 2048], P(None, 'tp'), may hold values from -0.625 to 0.625
- out_weight: bfloat16 [2048, 2048], P('tp', 'fsdp'), may hold values from -0.75 to 0.75
- out_bias: float32 [2048], replicated, may hold values from -1.75 to 1.75
- ln2_gain: float32 [2048], replicated, may hold values from 0.1 to 1.9
- ln2_bias: float32 [2048], replicated, may hold values from -1.75 to 1.75
- up_weight: bfloat16 [2048, 8192], P('fsdp', 'tp'), may hold values from -0.125 to 0.125
- up_bias: float32 [8192], P('tp'), may hold values from -1.75 to 1.75
- down_weight: bfloat16 [8192, 2048], P('tp', 'fsdp'), may hold values from -0.0625 to 0.0625
- down_bias: float32 [2048], replicated, may hold values from -1.75 to 1.75
- out_grad: bfloat16 [8192, 2048], P(('fsdp', 'tp')), may hold values from -6 to 6
Outputs:
- layer_out: bfloat16 [8192, 2048], P(('fsdp', 'tp'))
- tokens_grad: bfloat16 [8192, 2048], P(('fsdp', 'tp'))
- grad_ln1_gain: float32 [2048], replicated
- grad_ln1_bias: float32 [2048], replicated
- grad_qkv_weight: float32 [2048, 3, 2048], P('fsdp', None, 'tp')
- grad_qv_bias: float32 [2, 2048], P(None, 'tp')
- grad_out_weight: float32 [2048, 2048], P('tp', 'fsdp')
- grad_out_bias: float32 [2048], replicated
- grad_ln2_gain: float32 [2048], replicated
- grad_ln2_bias: float32 [2048], replicated
- grad_up_weight: float32 [2048, 8192], P('fsdp', 'tp')
- grad_up_bias: float32 [8192], P('tp')
- grad_down_weight: float32 [8192, 2048], P('tp', 'fsdp')
- grad_down_bias: float32 [2048], replicated
Inputs may be any that keep to these rules, and one draw needn't show every extreme that they name: `seq_group`: every group holds exactly two sequences. `seq_len`: every length is a multiple of 256; the two sequences of a group take at most 2048 rows together, and in every draw some group is filled exactly.
All inputs are finite; a program needn't handle non-finite values.
Results may differ from a plain program's by a relative error of at most 0.02.
Values may be sent and summed in bfloat16 or wider, within the bound.
No kernel may reach another device: no remote copies, remote signals or barrier semaphores. Data moves between devices by JAX's collectives and lax.ppermute only.
A program may use at most 192 MiB of HBM per device.

v0:
```python
import jax
import jax.numpy as jnp
from jax import lax
from jax.sharding import PartitionSpec as P

HEAD_DIM = 128


EPSILON = 1e-05
MASKED = -1e30


def layer_norm(values, gain_vec, bias_vec):
    row_mean = jnp.mean(values, axis=-1, keepdims=True)
    centred = values - row_mean
    variance = jnp.mean(centred * centred, axis=-1, keepdims=True)
    return centred * lax.rsqrt(variance + EPSILON) * gain_vec + bias_vec


def gelu_tanh(values):
    return jax.nn.gelu(values, approximate=True)


def row_keys(seq_len, seq_group, group_id, row_count):
    seq_count = seq_len.shape[0]
    seq_order = jnp.arange(seq_count, dtype=jnp.int32)
    same_before = (seq_group[None, :] == seq_group[:, None]) & (
        seq_order[None, :] < seq_order[:, None]
    )
    starts = jnp.sum(jnp.where(same_before, seq_len[None, :], 0), axis=1)
    places = jnp.arange(row_count, dtype=jnp.int32)[:, None]
    inside = (
        (seq_group[None, :] == group_id)
        & (starts[None, :] <= places)
        & (places < starts[None, :] + seq_len[None, :])
    )
    holder = jnp.sum(jnp.where(inside, seq_order[None, :] + 1, 0), axis=1)
    return jnp.where(holder > 0, holder - 1, seq_count + places[:, 0])


def contract_rows(left, right):
    return lax.dot_general(
        left, right, (((0,), (0,)), ((), ())), preferred_element_type=jnp.float32
    )


def contract_cols(left, right):
    return lax.dot_general(
        left, right, (((1,), (1,)), ((), ())), preferred_element_type=jnp.float32
    )


def local(
    tokens,
    seq_len,
    seq_group,
    ln1_gain,
    ln1_bias,
    qkv_weight,
    qv_bias,
    out_weight,
    out_bias,
    ln2_gain,
    ln2_bias,
    up_weight,
    up_bias,
    down_weight,
    down_bias,
    out_grad,
):
    tp_count = lax.axis_size("tp")
    tp_index = lax.axis_index("tp")
    own_rows = tokens.shape[0]
    all_rows = own_rows * tp_count
    width = tokens.shape[1]
    head_cols = qkv_weight.shape[2]
    local_heads = head_cols // HEAD_DIM
    ff_cols = up_weight.shape[1]
    scaling = HEAD_DIM ** (-0.5)
    blk_rows = min(512, all_rows)
    blk_count = all_rows // blk_rows
    group_keys = row_keys(seq_len, seq_group, lax.axis_index("fsdp"), all_rows)
    positions = jnp.arange(all_rows, dtype=jnp.int32)

    def gather_weights():
        return (
            lax.all_gather(qkv_weight, "fsdp", axis=0, tiled=True),
            lax.all_gather(out_weight, "fsdp", axis=1, tiled=True),
            lax.all_gather(up_weight, "fsdp", axis=0, tiled=True),
            lax.all_gather(down_weight, "fsdp", axis=1, tiled=True),
        )

    def block_scores(first_row, queries, keys_mat):
        q_block = lax.dynamic_slice_in_dim(queries, first_row, blk_rows, 0)
        query_keys = lax.dynamic_slice_in_dim(group_keys, first_row, blk_rows, 0)
        query_pos = lax.dynamic_slice_in_dim(positions, first_row, blk_rows, 0)
        allowed = (query_keys[:, None] == group_keys[None, :]) & (
            positions[None, :] <= query_pos[:, None]
        )
        scores = (
            jnp.einsum("qhd,khd->hqk", q_block, keys_mat, preferred_element_type=jnp.float32)
            * scaling
        )
        return (jnp.where(allowed[None], scores, MASKED), q_block)

    inputs = tokens.astype(jnp.float32)
    norm1 = layer_norm(inputs, ln1_gain, ln1_bias).astype(jnp.bfloat16)
    qkv_full, out_full, up_full, down_full = gather_weights()
    qkv_flat = qkv_full.reshape(width, 3 * head_cols)
    qkv_shift = jnp.concatenate([qv_bias[0], jnp.zeros_like(qv_bias[0]), qv_bias[1]])
    qkv_rows = (
        jnp.dot(
            lax.all_gather(norm1, "tp", axis=0, tiled=True),
            qkv_flat,
            preferred_element_type=jnp.float32,
        )
        + qkv_shift
    ).astype(jnp.bfloat16)
    queries = qkv_rows[:, :head_cols].reshape(all_rows, local_heads, HEAD_DIM)
    keys_mat = qkv_rows[:, head_cols : 2 * head_cols].reshape(all_rows, local_heads, HEAD_DIM)
    values = qkv_rows[:, 2 * head_cols :].reshape(all_rows, local_heads, HEAD_DIM)

    def attend_block(block_id):
        scores, q_block = block_scores(block_id * blk_rows, queries, keys_mat)
        top_score = jnp.max(scores, axis=-1, keepdims=True)
        weights = jnp.exp(scores - top_score)
        weight_sum = jnp.sum(weights, axis=-1, keepdims=True)
        probs = weights / weight_sum
        context_blk = jnp.einsum(
            "hqk,khd->qhd", probs.astype(jnp.bfloat16), values, preferred_element_type=jnp.float32
        )
        return (
            context_blk.astype(jnp.bfloat16).reshape(blk_rows, head_cols),
            (top_score + jnp.log(weight_sum))[..., 0],
        )

    ctx_blocks, lse_blocks = lax.map(attend_block, jnp.arange(blk_count))
    context = ctx_blocks.reshape(all_rows, head_cols)
    attn_rows = lax.psum_scatter(
        jnp.dot(context, out_full, preferred_element_type=jnp.float32).astype(jnp.bfloat16),
        "tp",
        scatter_dimension=0,
        tiled=True,
    ).astype(jnp.float32)
    middle = inputs + attn_rows + out_bias
    norm2 = layer_norm(middle, ln2_gain, ln2_bias).astype(jnp.bfloat16)
    pre = (
        jnp.dot(
            lax.all_gather(norm2, "tp", axis=0, tiled=True),
            up_full,
            preferred_element_type=jnp.float32,
        )
        + up_bias
    )
    act_rows = gelu_tanh(pre).astype(jnp.bfloat16)
    mlp_rows = lax.psum_scatter(
        jnp.dot(act_rows, down_full, preferred_element_type=jnp.float32).astype(jnp.bfloat16),
        "tp",
        scatter_dimension=0,
        tiled=True,
    ).astype(jnp.float32)
    layer_out = (middle + mlp_rows + down_bias).astype(jnp.bfloat16)
    grad_rows = out_grad.astype(jnp.float32)
    qkv_full, out_full, up_full, down_full = gather_weights()
    qkv_flat = qkv_full.reshape(width, 3 * head_cols)
    grad_piece = lax.all_gather(out_grad, "tp", axis=0, tiled=True)
    norm_piece = lax.all_gather(norm2, "tp", axis=0, tiled=True)
    pre = jnp.dot(norm_piece, up_full, preferred_element_type=jnp.float32) + up_bias
    act_value, gelu_back = jax.vjp(gelu_tanh, pre)
    act_piece = act_value.astype(jnp.bfloat16)
    down_acc = contract_rows(act_piece, grad_piece)
    act_grad = contract_cols(grad_piece, down_full)
    pre_grad = gelu_back(act_grad)[0].astype(jnp.bfloat16)
    up_acc = contract_rows(norm_piece, pre_grad)
    shift_acc = jnp.sum(pre_grad.astype(jnp.float32), axis=0)
    norm2_grad = lax.psum_scatter(
        contract_cols(pre_grad, up_full).astype(jnp.bfloat16), "tp", scatter_dimension=0, tiled=True
    ).astype(jnp.float32)
    unused_two, ln2_back = jax.vjp(layer_norm, middle, ln2_gain, ln2_bias)
    middle_ln, grad_g2, grad_b2 = ln2_back(norm2_grad)
    middle_grad = grad_rows + middle_ln
    proj_grad = middle_grad.astype(jnp.bfloat16)
    portion = lax.all_gather(proj_grad, "tp", axis=0, tiled=True)
    out_acc = contract_rows(context, portion)
    ctx_grad_rows = contract_cols(portion, out_full).astype(jnp.bfloat16)
    ctx_grads = ctx_grad_rows
    grad_out_w, ctx_grads = (out_acc, ctx_grads)
    ctx_grad = ctx_grads.reshape(all_rows, local_heads, HEAD_DIM)

    def attend_back(carried, block_id):
        key_acc, value_acc = carried
        first_row = block_id * blk_rows
        scores, q_block = block_scores(first_row, queries, keys_mat)
        probs = jnp.exp(scores - lse_blocks[block_id][:, :, None])
        grad_block = lax.dynamic_slice_in_dim(ctx_grad, first_row, blk_rows, 0)
        value_acc = value_acc + jnp.einsum(
            "hqk,qhd->khd",
            probs.astype(jnp.bfloat16),
            grad_block,
            preferred_element_type=jnp.float32,
        )
        prob_grad = jnp.einsum(
            "qhd,khd->hqk", grad_block, values, preferred_element_type=jnp.float32
        )
        row_dot = jnp.sum(probs * prob_grad, axis=-1, keepdims=True)
        score_grad = (probs * (prob_grad - row_dot)).astype(jnp.bfloat16)
        query_grad = (
            jnp.einsum("hqk,khd->qhd", score_grad, keys_mat, preferred_element_type=jnp.float32)
            * scaling
        )
        key_acc = (
            key_acc
            + jnp.einsum("hqk,qhd->khd", score_grad, q_block, preferred_element_type=jnp.float32)
            * scaling
        )
        return ((key_acc, value_acc), query_grad.astype(jnp.bfloat16).reshape(blk_rows, head_cols))

    acc_start = (
        jnp.zeros((all_rows, local_heads, HEAD_DIM), jnp.float32),
        jnp.zeros((all_rows, local_heads, HEAD_DIM), jnp.float32),
    )
    (key_acc, value_acc), query_grads = lax.scan(attend_back, acc_start, jnp.arange(blk_count))
    query_part = query_grads.reshape(all_rows, head_cols)
    value_part = value_acc.reshape(all_rows, head_cols).astype(jnp.bfloat16)
    qkv_grad = jnp.concatenate(
        [query_part, key_acc.reshape(all_rows, head_cols).astype(jnp.bfloat16), value_part], axis=1
    )
    qv_sums = jnp.stack(
        [
            jnp.sum(query_part.astype(jnp.float32), axis=0),
            jnp.sum(value_part.astype(jnp.float32), axis=0),
        ]
    )
    norm1_grad = lax.psum_scatter(
        contract_cols(qkv_grad, qkv_flat).astype(jnp.bfloat16),
        "tp",
        scatter_dimension=0,
        tiled=True,
    ).astype(jnp.float32)
    unused_one, ln1_back = jax.vjp(layer_norm, inputs, ln1_gain, ln1_bias)
    input_ln, grad_g1, grad_b1 = ln1_back(norm1_grad)
    tokens_grad = (middle_grad + input_ln).astype(jnp.bfloat16)
    grad_qkv_flat = contract_rows(lax.all_gather(norm1, "tp", axis=0, tiled=True), qkv_grad)
    grad_qkv_w = grad_qkv_flat.reshape(width, 3, head_cols)
    shard_qkv, shard_out, shard_up, shard_down = (
        lax.psum_scatter(
            grad_qkv_w.astype(jnp.bfloat16), "fsdp", scatter_dimension=0, tiled=True
        ).astype(jnp.float32),
        lax.psum_scatter(
            grad_out_w.astype(jnp.bfloat16), "fsdp", scatter_dimension=1, tiled=True
        ).astype(jnp.float32),
        lax.psum_scatter(
            up_acc.astype(jnp.bfloat16), "fsdp", scatter_dimension=0, tiled=True
        ).astype(jnp.float32),
        lax.psum_scatter(
            down_acc.astype(jnp.bfloat16), "fsdp", scatter_dimension=1, tiled=True
        ).astype(jnp.float32),
    )
    full_qv = lax.dynamic_update_slice(
        jnp.zeros((2, head_cols * tp_count), jnp.float32), qv_sums, (0, tp_index * head_cols)
    )
    full_up = lax.dynamic_update_slice_in_dim(
        jnp.zeros((ff_cols * tp_count,), jnp.float32), shift_acc, tp_index * ff_cols, 0
    )
    summed = lax.psum(
        (
            grad_g1,
            grad_b1,
            jnp.sum(middle_grad, axis=0),
            grad_g2,
            grad_b2,
            jnp.sum(grad_rows, axis=0),
            full_qv,
            full_up,
        ),
        ("fsdp", "tp"),
    )
    grad_qv = lax.dynamic_slice(summed[6], (0, tp_index * head_cols), (2, head_cols))
    grad_upb_own = lax.dynamic_slice_in_dim(summed[7], tp_index * ff_cols, ff_cols, 0)
    return (
        layer_out,
        tokens_grad,
        summed[0],
        summed[1],
        shard_qkv,
        grad_qv,
        shard_out,
        summed[2],
        summed[3],
        summed[4],
        shard_up,
        grad_upb_own,
        shard_down,
        summed[5],
    )


def solution(mesh):
    placed = (
        P(("fsdp", "tp"), None),
        P(),
        P(),
        P(),
        P(),
        P("fsdp", None, "tp"),
        P(None, "tp"),
        P("tp", "fsdp"),
        P(),
        P(),
        P(),
        P("fsdp", "tp"),
        P("tp"),
        P("tp", "fsdp"),
        P(),
        P(("fsdp", "tp"), None),
    )
    return jax.shard_map(
        local,
        mesh=mesh,
        in_specs=placed,
        out_specs=(
            P(("fsdp", "tp"), None),
            P(("fsdp", "tp"), None),
            P(),
            P(),
            P("fsdp", None, "tp"),
            P(None, "tp"),
            P("tp", "fsdp"),
            P(),
            P(),
            P(),
            P("fsdp", "tp"),
            P("tp"),
            P("tp", "fsdp"),
            P(),
        ),
        check_vma=False,
    )
```

profile of v0, /device:TPU:0, one launch (start us, length us, event | category | flops | bytes accessed | tf_op | source)
XLA Modules:
  0.0 1264.5 jit_solution(1588807803155996195)
XLA Ops:
  16.7 59.7 %all-gather.11.cloned.1.call-done = bf16[2048,3,256]{0,2,1:T(8,128)(2,1)} async-done(((bf16[512,3,256]{0,2,1:T(8,128)(2,1)}), bf16[2048,3,256]{0,2,1:T(8,128)(2,1)}) %all-gather.11.cloned.1.call-update) | async-done | bytes 3145744 | tf_op jit(solution)/shard_map/all_gather | solution.py:87
  76.4 55.4 %all-gather.9.cloned.1.call-done = bf16[2048,2048]{1,0:T(8,128)(2,1)} async-done(((bf16[256,2048]{1,0:T(8,128)(2,1)}), bf16[2048,2048]{1,0:T(8,128)(2,1)}) %all-gather.9.cloned.1.call-update) | async-done | bytes 8388624 | tf_op jit(solution)/shard_map/all_gather | solution.py:113
  146.8 47.2 %while.29 = (s32[]{:T(128)}, bf16[4,512,256]{2,1,0:T(8,128)(2,1)}, f32[4,2,512]{2,1,0:T(2,128)S(1)}, s32[4]{0:T(128)S(1)}, s32[2048]{0:T(1024)S(1)}, /*index=5*/...) while((s32[]{:T(128)}, bf16[4,512,256]{2,1,0:T(8,128)(2,1)}, ...), condition=%wide.region_7.8_spmd.clone, body=%wide.region_4.7_spmd.clone.sunk | while | flops 1102183424 | bytes 37286128 | solution.py:137
  202.4 70.8 %reduce-scatter.9.cloned.1.call-done = bf16[256,2048]{1,0:T(8,128)(2,1)} async-done(((bf16[2048,2048]{1,0:T(8,128)(2,1)}), bf16[256,2048]{1,0:T(8,128)(2,1)}) %reduce-scatter.9.cloned.1.call-update) | async-done | bytes 1048592 | tf_op jit(solution)/shard_map/reduce_scatter | solution.py:139
  280.0 75.4 %all-gather.17.cloned.1.call-done = bf16[2048,1024]{1,0:T(8,128)(2,1)} async-done(((bf16[512,1024]{1,0:T(8,128)(2,1)}), bf16[2048,1024]{1,0:T(8,128)(2,1)}) %all-gather.17.cloned.1.call-update) | async-done | bytes 4194320 | tf_op jit(solution)/shard_map/all_gather | solution.py:89
  355.4 55.1 %all-gather.15.cloned.1.call-done = bf16[2048,2048]{1,0:T(8,128)(2,1)} async-done(((bf16[256,2048]{1,0:T(8,128)(2,1)}), bf16[2048,2048]{1,0:T(8,128)(2,1)}) %all-gather.15.cloned.1.call-update) | async-done | bytes 8388624 | tf_op jit(solution)/shard_map/all_gather | solution.py:149
  410.5 14.4 %fusion.72 = f32[2048,1024]{1,0:T(8,128)} fusion(bf16[2048,2048]{1,0:T(8,128)(2,1)} %all-gather.15.cloned.1.call-done, bf16[2048,1024]{1,0:T(8,128)(2,1)} %all-gather.17.cloned.1.call-done), kind=kOutput, calls=%fused_computation.133 | convolution fusion | flops 8589934592 | bytes 20971520 | tf_op jit(solution)/shard_map/dot_general | solution.py:148
  424.8 68.0 %all-gather.19.cloned.1.call-done = bf16[1024,2048]{1,0:T(8,128)(2,1)} async-done(((bf16[1024,512]{1,0:T(8,128)(2,1)}), bf16[1024,2048]{1,0:T(8,128)(2,1)}) %all-gather.19.cloned.1.call-update) | async-done | bytes 4194320 | tf_op jit(solution)/shard_map/all_gather | solution.py:90
  492.8 54.7 %all-gather.21.cloned.1.call-done = bf16[2048,2048]{1,0:T(8,128)(2,1)} async-done(((bf16[256,2048]{1,0:T(8,128)(2,1)}), bf16[2048,2048]{1,0:T(8,128)(2,1)}) %all-gather.21.cloned.1.call-update) | async-done | bytes 8388624 | tf_op jit(solution)/shard_map/all_gather | solution.py:166
  547.5 20.8 %convert_reduce_fusion = (f32[1024]{0:T(1024)}, bf16[2048,1024]{1,0:T(8,128)(2,1)S(1)}) fusion(f32[2048,1024]{1,0:T(8,128)} %fusion.72, f32[1024]{0:T(1024)S(1)} %copy-done.33, bf16[2048,2048]{1,0:T(8,128)(2,1)} %all-gather.21.cloned.1.call-done, bf16[1024,2048]{1,0:T(8,128)(2,1)} %all-gather.19.cloned.1.call-done), kind=kOutput, calls=%fused_computation.52 | convolution fusion | flops 8638168064 | bytes 25174016 | tf_op jit(solution)/shard_map/dot_general | solution.py:48
  570.3 11.1 convolution_convert_fusion.1
  581.5 15.5 %convolution_convert_fusion.2 = bf16[2048,2048]{1,0:T(8,128)(2,1)} fusion(bf16[1024,2048]{1,0:T(8,128)(2,1)} %all-gather.19.cloned.1.call-done, f32[2048,1024]{1,0:T(8,128)} %fusion.72, f32[1024]{0:T(1024)S(1)} %copy-done.33), kind=kOutput, calls=%fused_computation.56 | convolution fusion | flops 8615100416 | bytes 20975616 | tf_op jit(solution)/shard_map/dot_general | solution.py:157
  597.1 56.0 %reduce-scatter.13.cloned.1.call-done = bf16[256,2048]{1,0:T(8,128)(2,1)} async-done(((bf16[2048,2048]{1,0:T(8,128)(2,1)}), bf16[256,2048]{1,0:T(8,128)(2,1)}) %reduce-scatter.13.cloned.1.call-update) | async-done | bytes 1048592 | tf_op jit(solution)/shard_map/reduce_scatter | solution.py:176
  658.9 69.0 %reduce-scatter.11.cloned.1.call-done = bf16[256,2048]{1,0:T(8,128)(2,1)} async-done(((bf16[2048,2048]{1,0:T(8,128)(2,1)}), bf16[256,2048]{1,0:T(8,128)(2,1)}) %reduce-scatter.11.cloned.1.call-update) | async-done | bytes 1048592 | tf_op jit(solution)/shard_map/reduce_scatter | solution.py:156
  735.4 16.9 %convolution_convert_fusion.4 = bf16[1024,2048]{1,0:T(8,128)(2,1)} fusion(bf16[2048,2048]{1,0:T(8,128)(2,1)} %all-gather.21.cloned.1.call-done, f32[2048,1024]{1,0:T(8,128)} %fusion.72, f32[1024]{0:T(1024)S(1)} %copy-done.33), kind=kOutput, calls=%fused_computation.59 | convolution fusion | flops 8613003264 | bytes 20975616 | tf_op jit(solution)/shard_map/dot_general | solution.py:42
  752.4 14.0 %convolution_convert_fusion.5 = bf16[2048,1024]{1,0:T(8,128)(2,1)} fusion(bf16[2048,2048]{1,0:T(8,128)(2,1)} %all-gather.15.cloned.1.call-done, bf16[2048,1024]{1,0:T(8,128)(2,1)} %copy-done.34), kind=kOutput, calls=%fused_computation.60 | convolution fusion | flops 8592031744 | bytes 16777216 | tf_op jit(solution)/shard_map/dot_general | solution.py:42
  768.9 20.9 %all-gather.23.cloned.1.call-done = bf16[2048,2048]{1,0:T(8,128)(2,1)} async-done(((bf16[256,2048]{1,0:T(8,128)(2,1)}), bf16[2048,2048]{1,0:T(8,128)(2,1)}) %all-gather.23.cloned.1.call-update) | async-done | bytes 8388624 | tf_op jit(solution)/shard_map/all_gather | solution.py:183
  804.6 89.1 %while.30 = (s32[]{:T(128)}, f32[2048,2,128]{0,2,1:T(8,128)S(1)}, f32[2048,2,128]{0,2,1:T(8,128)}, bf16[4,512,256]{1,2,0:T(8,128)(2,1)}, s32[4]{0:T(128)S(1)}, /...) while((s32[]{:T(128)}, f32[2048,2,128]{0,2,1:T(8,128)S(1)}, ...), condition=%wide.region_17.18_spmd.clone.clone, body=%wide.region_15.17_spmd.clone.clone.sunk | while | flops 2721840128 | bytes 88924512 | solution.py:222
  913.8 11.2 convolution_convert_fusion
  928.8 19.6 %reduce-scatter.21.cloned.1.call-done = bf16[512,1024]{1,0:T(8,128)(2,1)} async-done(((bf16[2048,1024]{1,0:T(8,128)(2,1)}), bf16[512,1024]{1,0:T(8,128)(2,1)}) %reduce-scatter.21.cloned.1.call-update) | async-done | bytes 1048592 | tf_op jit(solution)/shard_map/reduce_scatter | solution.py:252
  952.8 25.6 %reduce-scatter.19.cloned.1.call-done = bf16[256,512]{1,0:T(8,128)(2,1)} async-done(((bf16[256,2048]{1,0:T(8,128)(2,1)}), bf16[256,512]{1,0:T(8,128)(2,1)}) %reduce-scatter.19.cloned.1.call-update) | async-done | bytes 262160 | tf_op jit(solution)/shard_map/reduce_scatter | solution.py:249
  980.2 59.3 %reduce-scatter.17.cloned.1.call-done = bf16[512,3,256]{2,0,1:T(8,128)(2,1)} async-done(((bf16[2048,3,256]{2,0,1:T(8,128)(2,1)}), bf16[512,3,256]{2,0,1:T(8,128)(2,1)}) %reduce-scatter.17.cloned.1.call-update) | async-done | bytes 786448 | tf_op jit(solution)/shard_map/reduce_scatter | solution.py:246
  1041.8 72.3 %reduce-scatter.15.cloned.1.call-done = bf16[256,2048]{1,0:T(8,128)(2,1)} async-done(((bf16[2048,2048]{1,0:T(8,128)(2,1)}), bf16[256,2048]{1,0:T(8,128)(2,1)}) %reduce-scatter.15.cloned.1.call-update) | async-done | bytes 1048592 | tf_op jit(solution)/shard_map/reduce_scatter | solution.py:234
  1122.6 124.9 %all-reduce.3.cloned.1.call-done = (f32[2048]{0:T(1024)}, f32[2048]{0:T(1024)}, f32[2,2048]{1,0:T(2,128)}, f32[2048]{0:T(1024)}, f32[2048]{0:T(1024)}, /*index=5*/f32[2048]{0:T(1024)}, f32[8192]{0:T(1024)}, f32[2048]{0:T(1024)}) async-done(((f32[2048]{0:T(1024)}, f32[2048]{0:T(1024)}, f32[2,2048]{1,0:T(2,128)}, f32[2048]{0:T(1024)}, f32[2048]{0:T(1024)}, /*index=5*/f32[2048]{0:T(1024)}, f32[8192]{0:T(1024)}, ...) | async-done | bytes 98320 | tf_op jit(solution)/shard_map/psum | solution.py:265
  (284 shorter events, 246.0 us)
Async XLA Ops:
  7.2 69.1 %all-gather.11.cloned.1.call-start = ((), (), s32[]{:S(2)}) async-start(), calls=%async_computation.9 | async-start | bytes 3932160 | tf_op jit(solution)/shard_map/all_gather | solution.py:87
  9.7 122.1 %all-gather.9.cloned.1.call-start = ((), (), s32[]{:S(2)}) async-start(), calls=%async_computation.8 | async-start | bytes 9437184 | tf_op jit(solution)/shard_map/all_gather | solution.py:113
  15.4 178.6 %all-gather.13.cloned.1.call-start = ((), (), s32[]{:S(2)}) async-start(), calls=%async_computation.10 | async-start | bytes 1310720 | tf_op jit(solution)/shard_map/all_gather | solution.py:88
  16.2 257.0 %reduce-scatter.9.cloned.1.call-start = ((), (), s32[]{:S(2)}) async-start(), calls=%async_computation.11 | async-start | bytes 9437184 | tf_op jit(solution)/shard_map/reduce_scatter | solution.py:139
  201.5 153.8 %all-gather.17.cloned.1.call-start = ((), (), s32[]{:S(2)}) async-start(), calls=%async_computation.13 | async-start | bytes 5242880 | tf_op jit(solution)/shard_map/all_gather | solution.py:89
  202.1 208.3 %all-gather.15.cloned.1.call-start = ((), (), s32[]{:S(2)}) async-start(), calls=%async_computation.12 | async-start | bytes 9437184 | tf_op jit(solution)/shard_map/all_gather | solution.py:149
  278.4 214.4 %all-gather.19.cloned.1.call-start = ((), (), s32[]{:S(2)}) async-start(), calls=%async_computation.14 | async-start | bytes 5242880 | tf_op jit(solution)/shard_map/all_gather | solution.py:90
  279.2 268.3 %all-gather.21.cloned.1.call-start = ((), (), s32[]{:S(2)}) async-start(), calls=%async_computation.16 | async-start | bytes 9437184 | tf_op jit(solution)/shard_map/all_gather | solution.py:166
  279.9 267.5 %copy-start.33 = (f32[1024]{0:T(1024)S(1)}, f32[1024]{0:T(1024)}, u32[]{:S(2)}) copy-start(f32[1024]{0:T(1024)} %param.32) | copy-start | bytes 12292
  279.9 373.1 %reduce-scatter.13.cloned.1.call-start = ((), (), s32[]{:S(2)}) async-start(), calls=%async_computation.17 | async-start | bytes 9437184 | tf_op jit(solution)/shard_map/reduce_scatter | solution.py:176
  581.4 146.5 %reduce-scatter.11.cloned.1.call-start = ((), (), s32[]{:S(2)}) async-start(), calls=%async_computation.15 | async-start | bytes 9437184 | tf_op jit(solution)/shard_map/reduce_scatter | solution.py:156
  597.0 192.8 %all-gather.23.cloned.1.call-start = ((), (), s32[]{:S(2)}) async-start(), calls=%async_computation.18 | async-start | bytes 9437184 | tf_op jit(solution)/shard_map/all_gather | solution.py:183
  735.4 190.5 %reduce-scatter.23.cloned.1.call-start = ((), (), s32[]{:S(2)}) async-start(), calls=%async_computation.23 | async-start | bytes 5242880 | tf_op jit(solution)/shard_map/reduce_scatter | solution.py:255
  752.4 196.0 %reduce-scatter.21.cloned.1.call-start = ((), (), s32[]{:S(2)}) async-start(), calls=%async_computation.22 | async-start | bytes 5242880 | tf_op jit(solution)/shard_map/reduce_scatter | solution.py:252
  766.4 212.0 %reduce-scatter.19.cloned.1.call-start = ((), (), s32[]{:S(2)}) async-start(), calls=%async_computation.21 | async-start | bytes 1310720 | tf_op jit(solution)/shard_map/reduce_scatter | solution.py:249
  796.6 242.8 %reduce-scatter.17.cloned.1.call-start = ((), (), s32[]{:S(2)}) async-start(), calls=%async_computation.20 | async-start | bytes 3932160 | tf_op jit(solution)/shard_map/reduce_scatter | solution.py:246
  913.8 200.4 %reduce-scatter.15.cloned.1.call-start = ((), (), s32[]{:S(2)}) async-start(), calls=%async_computation.19 | async-start | bytes 9437184 | tf_op jit(solution)/shard_map/reduce_scatter | solution.py:234
  925.1 322.4 %all-reduce.3.cloned.1.call-start = ((), (), s32[]{:S(2)}) async-start(), calls=%async_computation.24 | async-start | bytes 196608 | tf_op jit(solution)/shard_map/psum | solution.py:265
  928.8 185.4 %copy-start.1 = (bf16[256,2048]{1,0:T(8,128)(2,1)S(1)}, bf16[256,2048]{1,0:T(8,128)(2,1)}, u32[]{:S(2)}) copy-start(bf16[256,2048]{1,0:T(8,128)(2,1)} %param.20) | copy-start | bytes 3145732
  928.8 185.4 %copy-start.16 = (f32[2048]{0:T(1024)S(1)}, f32[2048]{0:T(1024)}, u32[]{:S(2)}) copy-start(f32[2048]{0:T(1024)} %param.23) | copy-start | bytes 24580
  928.8 185.4 %copy-start.20 = (f32[256]{0:T(256)S(1)}, f32[256]{0:T(256)}, u32[]{:S(2)}) copy-start(f32[256]{0:T(256)} %copy-done.19) | copy-start | bytes 3076
  928.8 187.9 %copy-start.24 = (f32[256]{0:T(256)S(1)}, f32[256]{0:T(256)}, u32[]{:S(2)}) copy-start(f32[256]{0:T(256)} %copy-done.23) | copy-start | bytes 3076
  928.8 188.0 %copy-start.22 = (f32[256]{0:T(256)S(1)}, f32[256]{0:T(256)}, u32[]{:S(2)}) copy-start(f32[256]{0:T(256)} %copy-done.21) | copy-start | bytes 3076
  951.2 168.5 %copy-start.7 = (f32[256,2048]{1,0:T(8,128)S(1)}, f32[256,2048]{1,0:T(8,128)}, u32[]{:S(2)}) copy-start(f32[256,2048]{1,0:T(8,128)} %copy-done.6) | copy-start | bytes 6291460
  (37 other events, 873.0 us)
Sparse Core Ops, SparseCore 0:
  10.2 66.1 all-gather.10
  78.9 52.8 all-gather.8
  133.4 27.9 all-gather.12
  201.6 71.4 reduce-scatter.8
  274.6 80.7 all-gather.16
  357.7 52.7 all-gather.14
  412.0 80.7 all-gather.18
  494.7 52.7 all-gather.20
  581.5 71.4 reduce-scatter.12
  656.4 71.4 reduce-scatter.10
  735.5 54.2 all-gather.22
  791.9 76.7 reduce-scatter.22
  871.1 77.2 reduce-scatter.20
  950.5 27.8 reduce-scatter.18
  980.5 58.8 reduce-scatter.16
  1042.8 71.3 reduce-scatter.14
  1121.6 125.8 all-reduce.2
where the time goes:
time: 1280 us; the launch traced here: 1260 us
  waiting for transfers between devices  889 us (69%)
  matrix products  229 us (18%)
  other arithmetic  71.8 us (6%)
  local copies, waits for them, and re-layouts  45.4 us (4%)
  between operations  14.6 us (1%)
  loops' own time  13.5 us (1%)
    psum x1, waiting for transfers between devices, local(): lax.psum((grad_g1, grad_b1, jnp.sum(middle_grad, axis=0), grad_g2, grad_b...  125 us
    all_gather x1, waiting for transfers between devices, gather_weights(): lax.all_gather(up_weight, 'fsdp', axis=0, tiled=True)  75.4 us
    reduce_scatter x1, waiting for transfers between devices, local(): lax.psum_scatter(contract_cols(qkv_grad, qkv_flat).astype(jnp.bfloat16),...  72.3 us
    reduce_scatter x1, waiting for transfers between devices, local(): lax.psum_scatter(jnp.dot(context, out_full, preferred_element_type=jnp.fl...  70.8 us
    reduce_scatter x1, waiting for transfers between devices, local(): lax.psum_scatter(jnp.dot(act_rows, down_full, preferred_element_type=jnp....  69 us
    all_gather x1, waiting for transfers between devices, gather_weights(): lax.all_gather(down_weight, 'fsdp', axis=1, tiled=True)  68 us
    all_gather x1, waiting for transfers between devices, gather_weights(): lax.all_gather(qkv_weight, 'fsdp', axis=0, tiled=True)  59.7 us
    reduce_scatter x1, waiting for transfers between devices, local(): lax.psum_scatter(grad_qkv_w.astype(jnp.bfloat16), 'fsdp', scatter_dimensi...  59.3 us
  transfers between devices with their start and end apart: 17, of which 15 were waited for; matrix products, arithmetic and copies ran while one was open for 22% of the time, Pallas kernels for 0%

commit v1 on v0

--- a/solution.py
+++ b/solution.py
@@ -47,6 +47,86 @@
 def contract_cols(left, right):
     return lax.dot_general(
         left, right, (((1,), (1,)), ((), ())), preferred_element_type=jnp.float32
+    )
+
+
+SWAP_TP = 8
+
+
+def exchange(piece, mask):
+    return lax.ppermute(piece, "tp", [(at, at ^ mask) for at in range(SWAP_TP)])
+
+
+def gather_rows(piece):
+    if lax.axis_size("tp") != SWAP_TP:
+        return lax.all_gather(piece, "tp", axis=0, tiled=True)
+    half = piece.shape[0] // 2
+    from_x = exchange(piece, 2)
+    from_y = exchange(piece, 4)
+    own_twin = exchange(piece, 1)
+    far_low = exchange(from_x[:half], 4)
+    far_high = exchange(from_y[half:], 2)
+    parts = [from_x, from_y, far_low, far_high]
+    twins = [exchange(part, 1) for part in parts]
+    return jnp.concatenate([piece, *parts, own_twin, *twins], axis=0)
+
+
+def add_low(left, right):
+    return (left.astype(jnp.float32) + right.astype(jnp.float32)).astype(jnp.bfloat16)
+
+
+def scatter_rows(product):
+    tp_count = lax.axis_size("tp")
+    if tp_count != SWAP_TP:
+        return lax.psum_scatter(product(0, None), "tp", scatter_dimension=0, tiled=True).astype(
+            jnp.float32
+        )
+    twin_part = product(1, 2)
+    own_part = product(0, 2)
+    rows = own_part.shape[0] // 4
+    half = rows // 2
+    both = add_low(own_part, exchange(twin_part, 1))
+    home, to_x, to_y, far = (both[at * rows : (at + 1) * rows] for at in range(4))
+    far_low = exchange(far[:half], 2)
+    far_high = exchange(far[half:], 4)
+    x_low = exchange(to_x[:half], 2)
+    y_high = exchange(to_y[half:], 4)
+    x_high = exchange(add_low(to_x[half:], far_high), 2)
+    y_low = exchange(add_low(to_y[:half], far_low), 4)
+    wide = [part.astype(jnp.float32) for part in (x_low, x_high, y_low, y_high)]
+    return (
+        home.astype(jnp.float32)
+        + jnp.concatenate(wide[:2], axis=0)
+        + jnp.concatenate(wide[2:], axis=0)
+    )
+
+
+def sum_over(vector, axis):
+    count = lax.axis_size(axis)
+    terms = [vector] + [
+        lax.ppermute(vector, axis, [(at, at ^ step) for at in range(count)])
+        for step in range(1, count)
+    ]
+    while len(terms) > 1:
+        terms = [terms[at] + terms[at + 1] for at in range(0, len(terms), 2)]
+    return terms[0]
+
+
+def block_places(tp_count, tp_index):
+    block_at = jnp.arange(tp_count, dtype=jnp.int32)
+    if tp_count != SWAP_TP:
+        return block_at
+    apart = block_at ^ tp_index
+    return (apart >> 1) + 4 * (apart & 1)
+
+
+def take_blocks(rows, places, block_rows):
+    return jnp.concatenate(
+        [
+            lax.dynamic_slice_in_dim(rows, places[at] * block_rows, block_rows, 0)
+            for at in range(places.shape[0])
+        ],
+        axis=0,
     )
 
 
@@ -81,6 +161,15 @@
     blk_count = all_rows // blk_rows
     group_keys = row_keys(seq_len, seq_group, lax.axis_index("fsdp"), all_rows)
     positions = jnp.arange(all_rows, dtype=jnp.int32)
+    places = block_places(tp_count, tp_index)
+    slot_at = jnp.arange(tp_count, dtype=jnp.int32)
+    holders = (2 * (slot_at % 4) + slot_at // 4) ^ tp_index if tp_count == SWAP_TP else slot_at
+
+    def rows_of(rows, first, parts):
+        if parts is None:
+            return rows
+        count = rows.shape[0] // parts
+        return rows[first * count : (first + 1) * count]
 
     def gather_weights():
         return (
@@ -108,14 +197,16 @@
     qkv_full, out_full, up_full, down_full = gather_weights()
     qkv_flat = qkv_full.reshape(width, 3 * head_cols)
     qkv_shift = jnp.concatenate([qv_bias[0], jnp.zeros_like(qv_bias[0]), qv_bias[1]])
+    norm1_rows = gather_rows(norm1)
     qkv_rows = (
         jnp.dot(
-            lax.all_gather(norm1, "tp", axis=0, tiled=True),
+            norm1_rows,
             qkv_flat,
             preferred_element_type=jnp.float32,
         )
         + qkv_shift
     ).astype(jnp.bfloat16)
+    qkv_rows = take_blocks(qkv_rows, places, own_rows)
     queries = qkv_rows[:, :head_cols].reshape(all_rows, local_heads, HEAD_DIM)
     keys_mat = qkv_rows[:, head_cols : 2 * head_cols].reshape(all_rows, local_heads, HEAD_DIM)
     values = qkv_rows[:, 2 * head_cols :].reshape(all_rows, local_heads, HEAD_DIM)
@@ -135,37 +226,32 @@
         )
 
     ctx_blocks, lse_blocks = lax.map(attend_block, jnp.arange(blk_count))
-    context = ctx_blocks.reshape(all_rows, head_cols)
-    attn_rows = lax.psum_scatter(
-        jnp.dot(context, out_full, preferred_element_type=jnp.float32).astype(jnp.bfloat16),
-        "tp",
-        scatter_dimension=0,
-        tiled=True,
-    ).astype(jnp.float32)
+    context = take_blocks(ctx_blocks.reshape(all_rows, head_cols), holders, own_rows)
+    attn_rows = scatter_rows(
+        lambda first, parts: jnp.dot(
+            rows_of(context, first, parts), out_full, preferred_element_type=jnp.float32
+        ).astype(jnp.bfloat16)
+    )
     middle = inputs + attn_rows + out_bias
     norm2 = layer_norm(middle, ln2_gain, ln2_bias).astype(jnp.bfloat16)
+    norm_piece = gather_rows(norm2)
     pre = (
         jnp.dot(
-            lax.all_gather(norm2, "tp", axis=0, tiled=True),
+            norm_piece,
             up_full,
             preferred_element_type=jnp.float32,
         )
         + up_bias
     )
     act_rows = gelu_tanh(pre).astype(jnp.bfloat16)
-    mlp_rows = lax.psum_scatter(
-        jnp.dot(act_rows, down_full, preferred_element_type=jnp.float32).astype(jnp.bfloat16),
-        "tp",
-        scatter_dimension=0,
-        tiled=True,
-    ).astype(jnp.float32)
+    mlp_rows = scatter_rows(
+        lambda first, parts: jnp.dot(
+            rows_of(act_rows, first, parts), down_full, preferred_element_type=jnp.float32
+        ).astype(jnp.bfloat16)
+    )
     layer_out = (middle + mlp_rows + down_bias).astype(jnp.bfloat16)
     grad_rows = out_grad.astype(jnp.float32)
-    qkv_full, out_full, up_full, down_full = gather_weights()
-    qkv_flat = qkv_full.reshape(width, 3 * head_cols)
-    grad_piece = lax.all_gather(out_grad, "tp", axis=0, tiled=True)
-    norm_piece = lax.all_gather(norm2, "tp", axis=0, tiled=True)
-    pre = jnp.dot(norm_piece, up_full, preferred_element_type=jnp.float32) + up_bias
+    grad_piece = gather_rows(out_grad)
     act_value, gelu_back = jax.vjp(gelu_tanh, pre)
     act_piece = act_value.astype(jnp.bfloat16)
     down_acc = contract_rows(act_piece, grad_piece)
@@ -173,17 +259,19 @@
     pre_grad = gelu_back(act_grad)[0].astype(jnp.bfloat16)
     up_acc = contract_rows(norm_piece, pre_grad)
     shift_acc = jnp.sum(pre_grad.astype(jnp.float32), axis=0)
-    norm2_grad = lax.psum_scatter(
-        contract_cols(pre_grad, up_full).astype(jnp.bfloat16), "tp", scatter_dimension=0, tiled=True
-    ).astype(jnp.float32)
+    norm2_grad = scatter_rows(
+        lambda first, parts: contract_cols(rows_of(pre_grad, first, parts), up_full).astype(
+            jnp.bfloat16
+        )
+    )
     unused_two, ln2_back = jax.vjp(layer_norm, middle, ln2_gain, ln2_bias)
     middle_ln, grad_g2, grad_b2 = ln2_back(norm2_grad)
     middle_grad = grad_rows + middle_ln
     proj_grad = middle_grad.astype(jnp.bfloat16)
-    portion = lax.all_gather(proj_grad, "tp", axis=0, tiled=True)
+    portion = gather_rows(proj_grad)
     out_acc = contract_rows(context, portion)
     ctx_grad_rows = contract_cols(portion, out_full).astype(jnp.bfloat16)
-    ctx_grads = ctx_grad_rows
+    ctx_grads = take_blocks(ctx_grad_rows, places, own_rows)
     grad_out_w, ctx_grads = (out_acc, ctx_grads)
     ctx_grad = ctx_grads.reshape(all_rows, local_heads, HEAD_DIM)
 
@@ -225,22 +313,22 @@
     qkv_grad = jnp.concatenate(
         [query_part, key_acc.reshape(all_rows, head_cols).astype(jnp.bfloat16), value_part], axis=1
     )
+    qkv_grad = take_blocks(qkv_grad, holders, own_rows)
     qv_sums = jnp.stack(
         [
             jnp.sum(query_part.astype(jnp.float32), axis=0),
             jnp.sum(value_part.astype(jnp.float32), axis=0),
         ]
     )
-    norm1_grad = lax.psum_scatter(
-        contract_cols(qkv_grad, qkv_flat).astype(jnp.bfloat16),
-        "tp",
-        scatter_dimension=0,
-        tiled=True,
-    ).astype(jnp.float32)
+    norm1_grad = scatter_rows(
+        lambda first, parts: contract_cols(rows_of(qkv_grad, first, parts), qkv_flat).astype(
+            jnp.bfloat16
+        )
+    )
     unused_one, ln1_back = jax.vjp(layer_norm, inputs, ln1_gain, ln1_bias)
     input_ln, grad_g1, grad_b1 = ln1_back(norm1_grad)
     tokens_grad = (middle_grad + input_ln).astype(jnp.bfloat16)
-    grad_qkv_flat = contract_rows(lax.all_gather(norm1, "tp", axis=0, tiled=True), qkv_grad)
+    grad_qkv_flat = contract_rows(norm1_rows, qkv_grad)
     grad_qkv_w = grad_qkv_flat.reshape(width, 3, head_cols)
     shard_qkv, shard_out, shard_up, shard_down = (
         lax.psum_scatter(
@@ -256,42 +344,32 @@
             down_acc.astype(jnp.bfloat16), "fsdp", scatter_dimension=1, tiled=True
         ).astype(jnp.float32),
     )
-    full_qv = lax.dynamic_update_slice(
-        jnp.zeros((2, head_cols * tp_count), jnp.float32), qv_sums, (0, tp_index * head_cols)
-    )
-    full_up = lax.dynamic_update_slice_in_dim(
-        jnp.zeros((ff_cols * tp_count,), jnp.float32), shift_acc, tp_index * ff_cols, 0
-    )
-    summed = lax.psum(
-        (
-            grad_g1,
-            grad_b1,
-            jnp.sum(middle_grad, axis=0),
-            grad_g2,
-            grad_b2,
-            jnp.sum(grad_rows, axis=0),
-            full_qv,
-            full_up,
+    own_sums = sum_over(jnp.concatenate([qv_sums.reshape(-1), shift_acc]), "fsdp")
+    grad_qv = own_sums[: 2 * head_cols].reshape(2, head_cols)
+    grad_upb_own = own_sums[2 * head_cols :]
+    early = sum_over(
+        sum_over(
+            jnp.stack([jnp.sum(middle_grad, axis=0), grad_g2, grad_b2, jnp.sum(grad_rows, axis=0)]),
+            "fsdp",
         ),
-        ("fsdp", "tp"),
-    )
-    grad_qv = lax.dynamic_slice(summed[6], (0, tp_index * head_cols), (2, head_cols))
-    grad_upb_own = lax.dynamic_slice_in_dim(summed[7], tp_index * ff_cols, ff_cols, 0)
+        "tp",
+    )
+    late = sum_over(sum_over(jnp.stack([grad_g1, grad_b1]), "fsdp"), "tp")
     return (
         layer_out,
         tokens_grad,
-        summed[0],
-        summed[1],
+        late[0],
+        late[1],
         shard_qkv,
         grad_qv,
         shard_out,
-        summed[2],
-        summed[3],
-        summed[4],
+        early[0],
+        early[1],
+        early[2],
         shard_up,
         grad_upb_own,
         shard_down,
-        summed[5],
+        early[3],
     )
 
 

time: 1280 us -> 733 us (0.57)
  waiting for transfers between devices: 889 us -> 194 us
  local copies, waits for them, and re-layouts: 45.4 us -> 121 us
  starting transfers between devices: 1.04 us -> 74.3 us
    reduce_scatter x4 -> x0, waiting for transfers between devices: 268 us -> none  [the longest x1 72.3 us: local(): lax.psum_scatter(contract_cols(qkv_grad, qkv_flat).astype(jnp.bfloat16),...]
    ppermute x0 -> x87, waiting for transfers between devices: none -> 187 us  [the longest x64 183 us: exchange(): return lax.ppermute(piece, 'tp', [(at, at ^ mask) for at in range(SWAP_TP)])]
    all_gather x4 -> x0, waiting for transfers between devices: 186 us -> none  [the longest x1 55.4 us: local(): lax.all_gather(norm1, 'tp', axis=0, tiled=True)]
    psum x1 -> x0, waiting for transfers between devices: 125 us -> none  [local(): lax.psum((grad_g1, grad_b1, jnp.sum(middle_grad, axis=0), grad_g2, grad_b...]
    all_gather x1, waiting for transfers between devices: 75.4 us -> 0.01 us  [gather_weights(): lax.all_gather(up_weight, 'fsdp', axis=0, tiled=True)]
    ppermute x0 -> x87, starting transfers between devices: none -> 74 us  [the longest x64 53.4 us: exchange(): return lax.ppermute(piece, 'tp', [(at, at ^ mask) for at in range(SWAP_TP)])]
    all_gather x1, waiting for transfers between devices: 68 us -> 0.01 us  [gather_weights(): lax.all_gather(down_weight, 'fsdp', axis=1, tiled=True)]
    reduce_scatter x1, waiting for transfers between devices: 59.3 us -> 0.01 us  [local(): lax.psum_scatter(grad_qkv_w.astype(jnp.bfloat16), 'fsdp', scatter_dimensi...]
  transfers between devices with their start and end apart: 17 -> 95, of which waited for: 15 -> 29; matrix products, arithmetic and copies ran while one was open for 22% -> 51% of each run, Pallas kernels for 0% -> 0%
where the time goes in v1:
time: 733 us; the launch traced here: 721 us
  matrix products  221 us (30%)
  waiting for transfers between devices  194 us (26%)
  local copies, waits for them, and re-layouts  121 us (17%)
  starting transfers between devices  74.3 us (10%)
  other arithmetic  71 us (10%)
  between operations  25.9 us (4%)
  loops' own time  13.6 us (2%)
    ppermute x64, waiting for transfers between devices, exchange(): return lax.ppermute(piece, 'tp', [(at, at ^ mask) for at in range(SWAP_TP)])  183 us
    unnamed x160, local copies, waits for them, and re-layouts  71.6 us
    dot_general x6, matrix products, contract_cols(): lax.dot_general(left, right, (((1,), (1,)), ((), ())), preferred_element_...  59.1 us
    ppermute x64, starting transfers between devices, exchange(): return lax.ppermute(piece, 'tp', [(at, at ^ mask) for at in range(SWAP_TP)])  53.4 us
    dot_general x4, matrix products, contract_rows(): lax.dot_general(left, right, (((0,), (0,)), ((), ())), preferred_element_...  38.5 us
    dot_general x8, matrix products, block_scores(): jnp.einsum('qhd,khd->hqk', q_block, keys_mat, preferred_element_type=jnp....  23.4 us
    ppermute x23, starting transfers between devices, sum_over(): lax.ppermute(vector, axis, [(at, at ^ step) for at in range(count)])  20.6 us
    dot_general x4, matrix products, attend_back(): jnp.einsum('hqk,qhd->khd', probs.astype(jnp.bfloat16), grad_block, prefer...  18.4 us
  transfers between devices with their start and end apart: 95, of which 29 were waited for; matrix products, arithmetic and copies ran while one was open for 51% of the time, Pallas kernels for 0%

profile of v1, /device:TPU:0, one launch (start us, length us, event | category | flops | bytes accessed | tf_op | source)
XLA Modules:
  0.0 721.1 jit_solution(3369066888845294926)
XLA Ops:
  21.0 20.8 %collective-permute-done.1 = bf16[256,2048]{1,0:T(8,128)(2,1)S(1)} collective-permute-done((bf16[256,2048]{1,0:T(8,128)(2,1)}, bf16[256,2048]{1,0:T(8,128)(2,1)S(1)}, u32[]{:S(2)}, u32[]{:S(2)}) %collective-permute-start.1) | collective-permute-done | bytes 1048608 | tf_op jit(solution)/shard_map/ppermute | solution.py:57
  76.4 10.1 %add_convert_fusion.4 = bf16[2048,768]{1,0:T(8,128)(2,1)S(1)} fusion(f32[768]{0:T(1024)S(1)} %pad_maximum_fusion.4, bf16[2048,2048]{1,0:T(8,128)(2,1)} %constant_dynamic-update-slice_fusion.1, bf16[2048,768]{0,1:T(8,128)(2,1)} %bitcast.188), kind=kOutput, calls=%fused_computation.57 | convolution fusion | flops 6445596672 | bytes 14683136 | tf_op jit(solution)/shard_map/dot_general | solution.py:202
  91.5 49.7 %while.29 = (s32[]{:T(128)}, bf16[4,512,256]{2,1,0:T(8,128)(2,1)}, f32[4,2,512]{2,1,0:T(2,128)}, s32[4]{0:T(128)S(1)}, s32[2048]{0:T(1024)S(1)}, /*index=5*/s32[...) while((s32[]{:T(128)}, bf16[4,512,256]{2,1,0:T(8,128)(2,1)}, ...), condition=%wide.region_7.8_spmd.clone, body=%wide.region_4.7_spmd.clone.sunk | while | flops 1102183424 | bytes 37286128 | solution.py:228
  172.7 11.8 %collective-permute-done.32 = bf16[256,2048]{1,0:T(8,128)(2,1)} collective-permute-done((bf16[256,2048]{1,0:T(8,128)(2,1)}, bf16[256,2048]{1,0:T(8,128)(2,1)}, u32[]{:S(2)}, u32[]{:S(2)}) %collective-permute-start.32) | collective-permute-done | bytes 1048608 | tf_op jit(solution)/shard_map/ppermute | solution.py:57
  187.7 7.9 %collective-permute-done.13 = bf16[128,2048]{1,0:T(8,128)(2,1)S(1)} collective-permute-done((bf16[128,2048]{1,0:T(8,128)(2,1)}, bf16[128,2048]{1,0:T(8,128)(2,1)S(1)}, u32[]{:S(2)}, u32[]{:S(2)}) %collective-permute-start.13) | collective-permute-done | bytes 524320 | tf_op jit(solution)/shard_map/ppermute | solution.py:57
  208.3 8.3 %collective-permute-done.15 = bf16[128,2048]{1,0:T(8,128)(2,1)S(1)} collective-permute-done((bf16[128,2048]{1,0:T(8,128)(2,1)S(1)}, bf16[128,2048]{1,0:T(8,128)(2,1)S(1)}, u32[]{:S(2)}, u32[]{:S(2)}) %collective-permute-start.15) | collective-permute-done | bytes 524320 | tf_op jit(solution)/shard_map/ppermute | solution.py:57
  218.1 9.2 %collective-permute-done.14 = bf16[128,2048]{1,0:T(8,128)(2,1)S(1)} collective-permute-done((bf16[128,2048]{1,0:T(8,128)(2,1)S(1)}, bf16[128,2048]{1,0:T(8,128)(2,1)S(1)}, u32[]{:S(2)}, u32[]{:S(2)}) %collective-permute-start.14) | collective-permute-done | bytes 524320 | tf_op jit(solution)/shard_map/ppermute | solution.py:57
  236.4 19.5 %collective-permute-done.17 = bf16[256,2048]{1,0:T(8,128)(2,1)S(1)} collective-permute-done((bf16[256,2048]{1,0:T(8,128)(2,1)S(1)}, bf16[256,2048]{1,0:T(8,128)(2,1)S(1)}, u32[]{:S(2)}, u32[]{:S(2)}) %collective-permute-start.17) | collective-permute-done | bytes 1048608 | tf_op jit(solution)/shard_map/ppermute | solution.py:57
  276.7 14.8 %fusion.114 = f32[2048,1024]{1,0:T(8,128)} fusion(bf16[2048,2048]{1,0:T(8,128)(2,1)} %constant_dynamic-update-slice_fusion.11, bf16[2048,1024]{1,0:T(8,128)(2,1)} %all-gather.9.cloned.1.call-done), kind=kOutput, calls=%fused_computation.290 | convolution fusion | flops 8589934592 | bytes 20971520 | tf_op jit(solution)/shard_map/dot_general | solution.py:239
  291.5 21.8 %convert_reduce_fusion = (f32[1024]{0:T(1024)}, bf16[2048,1024]{1,0:T(8,128)(2,1)}, bf16[2048,1024]{1,0:T(8,128)(2,1)}) fusion(f32[2048,1024]{1,0:T(8,128)} %fusion.114, f32[1024]{0:T(1024)S(1)} %copy-done.42, bf16[2048,2048]{1,0:T(8,128)(2,1)} %copy-done.14, bf16[1024,2048]{1,0:T(8,128)(2,1)} %all-gather.11.cloned.1.call-done), kind=kOutput, calls=%fused_computation.51 | convolution fusion | flops 8642362368 | bytes 29368320 | tf_op jit(solution)/shard_map/dot_general | solution.py:48
  313.3 7.9 %convolution_convert_fusion.3 = bf16[1024,2048]{1,0:T(8,128)(2,1)} fusion(bf16[2048,1024]{1,0:T(8,128)(2,1)S(1)} %copy-done.38, bf16[2048,1024]{1,0:T(8,128)(2,1)} %get-tuple-element.357), kind=kOutput, calls=%fused_computation.61 | convolution fusion | flops 4297064448 | bytes 10485760 | tf_op jit(solution)/shard_map/dot_general | solution.py:48
  327.9 10.6 %convolution_convert_fusion = bf16[1024,2048]{1,0:T(8,128)(2,1)} fusion(bf16[2048,1024]{1,0:T(8,128)(2,1)S(1)} %copy-done.43, bf16[2048,2048]{1,0:T(8,128)(2,1)S(1)} %bitcast.163), kind=kOutput, calls=%fused_computation.58 | convolution fusion | flops 8592031744 | bytes 16777216 | tf_op jit(solution)/shard_map/dot_general | solution.py:42
  338.7 9.1 %add_convert_fusion.1 = bf16[1024,2048]{1,0:T(8,128)(2,1)S(1)} fusion(bf16[1024,2048]{1,0:T(8,128)(2,1)} %collective-permute-done.41, bf16[2048,1024]{1,0:T(8,128)(2,1)} %all-gather.9.cloned.1.call-done, bf16[2048,1024]{1,0:T(8,128)(2,1)} %get-tuple-element.357), kind=kOutput, calls=%fused_computation.53 | convolution fusion | flops 4305453056 | bytes 14680064 | tf_op jit(solution)/shard_map/dot_general | solution.py:48
  365.3 8.8 %collective-permute-done.29 = bf16[128,2048]{1,0:T(8,128)(2,1)S(1)} collective-permute-done((bf16[128,2048]{1,0:T(8,128)(2,1)S(1)}, bf16[128,2048]{1,0:T(8,128)(2,1)S(1)}, u32[]{:S(2)}, u32[]{:S(2)}) %collective-permute-start.29) | collective-permute-done | bytes 524320 | tf_op jit(solution)/shard_map/ppermute | solution.py:57
  376.5 8.8 %collective-permute-done.42 = bf16[128,2048]{1,0:T(8,128)(2,1)S(1)} collective-permute-done((bf16[128,2048]{1,0:T(8,128)(2,1)S(1)}, bf16[128,2048]{1,0:T(8,128)(2,1)S(1)}, u32[]{:S(2)}, u32[]{:S(2)}) %collective-permute-start.42) | collective-permute-done | bytes 524320 | tf_op jit(solution)/shard_map/ppermute | solution.py:57
  387.0 9.5 %collective-permute-done.44 = bf16[128,2048]{1,0:T(8,128)(2,1)S(1)} collective-permute-done((bf16[128,2048]{1,0:T(8,128)(2,1)S(1)}, bf16[128,2048]{1,0:T(8,128)(2,1)S(1)}, u32[]{:S(2)}, u32[]{:S(2)}) %collective-permute-start.44) | collective-permute-done | bytes 524320 | tf_op jit(solution)/shard_map/ppermute | solution.py:57
  398.9 9.6 %collective-permute-done.31 = bf16[128,2048]{1,0:T(8,128)(2,1)S(1)} collective-permute-done((bf16[128,2048]{1,0:T(8,128)(2,1)S(1)}, bf16[128,2048]{1,0:T(8,128)(2,1)S(1)}, u32[]{:S(2)}, u32[]{:S(2)}) %collective-permute-start.31) | collective-permute-done | bytes 524320 | tf_op jit(solution)/shard_map/ppermute | solution.py:57
  408.5 10.5 %collective-permute-done.30 = bf16[128,2048]{1,0:T(8,128)(2,1)S(1)} collective-permute-done((bf16[128,2048]{1,0:T(8,128)(2,1)S(1)}, bf16[128,2048]{1,0:T(8,128)(2,1)S(1)}, u32[]{:S(2)}, u32[]{:S(2)}) %collective-permute-start.30) | collective-permute-done | bytes 524320 | tf_op jit(solution)/shard_map/ppermute | solution.py:57
  433.3 18.5 %collective-permute-done.49 = bf16[256,2048]{1,0:T(8,128)(2,1)} collective-permute-done((bf16[256,2048]{1,0:T(8,128)(2,1)}, bf16[256,2048]{1,0:T(8,128)(2,1)}, u32[]{:S(2)}, u32[]{:S(2)}) %collective-permute-start.49) | collective-permute-done | bytes 1048608 | tf_op jit(solution)/shard_map/ppermute | solution.py:57
  458.3 14.0 %convolution_convert_fusion.5 = bf16[2048,1024]{1,0:T(8,128)(2,1)} fusion(bf16[2048,2048]{1,0:T(8,128)(2,1)} %constant_dynamic-update-slice_fusion.11, bf16[2048,1024]{1,0:T(8,128)(2,1)} %get-tuple-element.357), kind=kOutput, calls=%fused_computation.63 | convolution fusion | flops 8592031744 | bytes 16777216 | tf_op jit(solution)/shard_map/dot_general | solution.py:42
  501.9 95.3 %while.30 = (s32[]{:T(128)}, f32[2048,2,128]{0,2,1:T(8,128)S(1)}, f32[2048,2,128]{0,2,1:T(8,128)}, bf16[4,512,256]{1,2,0:T(8,128)(2,1)}, s32[4]{0:T(128)S(1)}, /...) while((s32[]{:T(128)}, f32[2048,2,128]{0,2,1:T(8,128)S(1)}, ...), condition=%wide.region_14.15_spmd.clone.clone, body=%wide.region_12.14_spmd.clone.clone.sunk | while | flops 2721840128 | bytes 85254464 | solution.py:310
  633.0 9.4 %convolution_convert_fusion.6 = bf16[2048,768]{0,1:T(8,128)(2,1)S(1)} fusion(bf16[2048,2048]{1,0:T(8,128)(2,1)} %constant_dynamic-update-slice_fusion.1, bf16[2048,768]{1,0:T(8,128)(2,1)S(1)} %copy-done.21), kind=kOutput, calls=%fused_computation.64 | convolution fusion | flops 6444023808 | bytes 14680064 | tf_op jit(solution)/shard_map/dot_general | solution.py:42
  652.4 8.2 %collective-permute-done.58 = bf16[128,2048]{1,0:T(8,128)(2,1)S(1)} collective-permute-done((bf16[128,2048]{1,0:T(8,128)(2,1)}, bf16[128,2048]{1,0:T(8,128)(2,1)S(1)}, u32[]{:S(2)}, u32[]{:S(2)}) %collective-permute-start.58) | collective-permute-done | bytes 524320 | tf_op jit(solution)/shard_map/ppermute | solution.py:57
  660.9 10.0 %collective-permute-done.60 = bf16[128,2048]{1,0:T(8,128)(2,1)S(1)} collective-permute-done((bf16[128,2048]{1,0:T(8,128)(2,1)S(1)}, bf16[128,2048]{1,0:T(8,128)(2,1)S(1)}, u32[]{:S(2)}, u32[]{:S(2)}) %collective-permute-start.60) | collective-permute-done | bytes 524320 | tf_op jit(solution)/shard_map/ppermute | solution.py:57
  (557 shorter events, 422.5 us)
Async XLA Ops:
  7.2 69.1 %all-gather.5.cloned.1.call-start = ((), (), s32[]{:S(2)}) async-start(), calls=%async_computation.4 | async-start | bytes 3932160 | tf_op jit(solution)/shard_map/all_gather | solution.py:176
  9.7 144.3 %all-gather.7.cloned.1.call-start = ((), (), s32[]{:S(2)}) async-start(), calls=%async_computation.5 | async-start | bytes 1310720 | tf_op jit(solution)/shard_map/all_gather | solution.py:177
  10.4 266.3 %all-gather.9.cloned.1.call-start = ((), (), s32[]{:S(2)}) async-start(), calls=%async_computation.6 | async-start | bytes 5242880 | tf_op jit(solution)/shard_map/all_gather | solution.py:178
  14.8 49.1 %collective-permute-start.4 = (bf16[256,2048]{1,0:T(8,128)(2,1)}, bf16[256,2048]{1,0:T(8,128)(2,1)}, u32[]{:S(2)}, u32[]{:S(2)}) collective-permute-start(bf16[256,2048]{1,0:T(8,128)(2,1)} %get-tuple-element.385), channel_id=1, source_target_pairs={{0,1},{1,0},{2,3},{3,2},{4,5},{5,4},{6,7},{7,6},{8,9},{9,8},{10,11... | collective-permute-start | bytes 3145736 | tf_op jit(solution)/shard_map/ppermute | solution.py:57
  15.3 26.5 %collective-permute-start.1 = (bf16[256,2048]{1,0:T(8,128)(2,1)}, bf16[256,2048]{1,0:T(8,128)(2,1)S(1)}, u32[]{:S(2)}, u32[]{:S(2)}) collective-permute-start(bf16[256,2048]{1,0:T(8,128)(2,1)} %get-tuple-element.385), channel_id=1, source_target_pairs={{0,4},{1,5},{2,6},{3,7},{4,0},{5,1},{6,2},{7,3},{8,12},{9,13},{10,... | collective-permute-start | bytes 3145736 | tf_op jit(solution)/shard_map/ppermute | solution.py:57
  17.8 26.6 %collective-permute-start = (bf16[256,2048]{1,0:T(8,128)(2,1)}, bf16[256,2048]{1,0:T(8,128)(2,1)S(1)}, u32[]{:S(2)}, u32[]{:S(2)}) collective-permute-start(bf16[256,2048]{1,0:T(8,128)(2,1)} %get-tuple-element.385), channel_id=1, source_target_pairs={{0,2},{1,3},{2,0},{3,1},{4,6},{5,7},{6,4},{7,5},{8,10},{9,11},{10,... | collective-permute-start | bytes 3145736 | tf_op jit(solution)/shard_map/ppermute | solution.py:57
  19.3 272.2 %all-gather.11.cloned.1.call-start = ((), (), s32[]{:S(2)}) async-start(), calls=%async_computation.7 | async-start | bytes 5242880 | tf_op jit(solution)/shard_map/all_gather | solution.py:179
  156.6 42.8 %collective-permute-start.33 = (bf16[256,2048]{1,0:T(8,128)(2,1)}, bf16[256,2048]{1,0:T(8,128)(2,1)}, u32[]{:S(2)}, u32[]{:S(2)}) collective-permute-start(bf16[256,2048]{1,0:T(8,128)(2,1)} %param.35), channel_id=1, source_target_pairs={{0,4},{1,5},{2,6},{3,7},{4,0},{5,1},{6,2},{7,3},{8,12},{9,13},{10,... | collective-permute-start | bytes 3145736 | tf_op jit(solution)/shard_map/ppermute | solution.py:57
  158.1 26.3 %collective-permute-start.32 = (bf16[256,2048]{1,0:T(8,128)(2,1)}, bf16[256,2048]{1,0:T(8,128)(2,1)}, u32[]{:S(2)}, u32[]{:S(2)}) collective-permute-start(bf16[256,2048]{1,0:T(8,128)(2,1)} %param.35), channel_id=1, source_target_pairs={{0,2},{1,3},{2,0},{3,1},{4,6},{5,7},{6,4},{7,5},{8,10},{9,11},{10,... | collective-permute-start | bytes 3145736 | tf_op jit(solution)/shard_map/ppermute | solution.py:57
  168.3 27.3 %collective-permute-start.13 = (bf16[128,2048]{1,0:T(8,128)(2,1)}, bf16[128,2048]{1,0:T(8,128)(2,1)S(1)}, u32[]{:S(2)}, u32[]{:S(2)}) collective-permute-start(bf16[128,2048]{1,0:T(8,128)(2,1)} %get-tuple-element.412), channel_id=1, source_target_pairs={{0,2},{1,3},{2,0},{3,1},{4,6},{5,7},{6,4},{7,5},{8,10},{9,11},{10,... | collective-permute-start | bytes 1572872 | tf_op jit(solution)/shard_map/ppermute | solution.py:57
  169.8 26.4 %collective-permute-start.11 = (bf16[128,2048]{1,0:T(8,128)(2,1)}, bf16[128,2048]{1,0:T(8,128)(2,1)S(1)}, u32[]{:S(2)}, u32[]{:S(2)}) collective-permute-start(bf16[128,2048]{1,0:T(8,128)(2,1)} %get-tuple-element.413), channel_id=1, source_target_pairs={{0,4},{1,5},{2,6},{3,7},{4,0},{5,1},{6,2},{7,3},{8,12},{9,13},{10,... | collective-permute-start | bytes 1572872 | tf_op jit(solution)/shard_map/ppermute | solution.py:57
  171.3 517.8 %reduce-scatter.11.cloned.1.call-start = ((), (), s32[]{:S(2)}) async-start(), calls=%async_computation.11 | async-start | bytes 5242880 | tf_op jit(solution)/shard_map/reduce_scatter | solution.py:343
  199.4 27.9 %collective-permute-start.14 = (bf16[128,2048]{1,0:T(8,128)(2,1)S(1)}, bf16[128,2048]{1,0:T(8,128)(2,1)S(1)}, u32[]{:S(2)}, u32[]{:S(2)}) collective-permute-start(bf16[128,2048]{1,0:T(8,128)(2,1)S(1)} %get-tuple-element.415), channel_id=1, source_target_pairs={{0,4},{1,5},{2,6},{3,7},{4,0},{5,1},{6,2},{7,3},{8,12},{9,13},{10,... | collective-permute-start | bytes 1572872 | tf_op jit(solution)/shard_map/ppermute | solution.py:57
  205.4 28.7 %collective-permute-start.36 = (bf16[256,2048]{1,0:T(8,128)(2,1)}, bf16[256,2048]{1,0:T(8,128)(2,1)S(1)}, u32[]{:S(2)}, u32[]{:S(2)}) collective-permute-start(bf16[256,2048]{1,0:T(8,128)(2,1)} %param.35), channel_id=1, source_target_pairs={{0,1},{1,0},{2,3},{3,2},{4,5},{5,4},{6,7},{7,6},{8,9},{9,8},{10,11... | collective-permute-start | bytes 3145736 | tf_op jit(solution)/shard_map/ppermute | solution.py:57
  236.2 35.6 %collective-permute-start.20 = (bf16[256,2048]{1,0:T(8,128)(2,1)S(1)}, bf16[256,2048]{1,0:T(8,128)(2,1)S(1)}, u32[]{:S(2)}, u32[]{:S(2)}) collective-permute-start(bf16[256,2048]{1,0:T(8,128)(2,1)S(1)} %get-tuple-element.381), channel_id=1, source_target_pairs={{0,1},{1,0},{2,3},{3,2},{4,5},{5,4},{6,7},{7,6},{8,9},{9,8},{10,11... | collective-permute-start | bytes 3145736 | tf_op jit(solution)/shard_map/ppermute | solution.py:57
  338.6 353.3 %reduce-scatter.9.cloned.1.call-start = ((), (), s32[]{:S(2)}) async-start(), calls=%async_computation.10 | async-start | bytes 5242880 | tf_op jit(solution)/shard_map/reduce_scatter | solution.py:340
  364.3 32.2 %collective-permute-start.44 = (bf16[128,2048]{1,0:T(8,128)(2,1)S(1)}, bf16[128,2048]{1,0:T(8,128)(2,1)S(1)}, u32[]{:S(2)}, u32[]{:S(2)}) collective-permute-start(bf16[128,2048]{1,0:T(8,128)(2,1)S(1)} %get-tuple-element.402), channel_id=1, source_target_pairs={{0,2},{1,3},{2,0},{3,1},{4,6},{5,7},{6,4},{7,5},{8,10},{9,11},{10,... | collective-permute-start | bytes 1572872 | tf_op jit(solution)/shard_map/ppermute | solution.py:57
  375.2 33.3 %collective-permute-start.31 = (bf16[128,2048]{1,0:T(8,128)(2,1)S(1)}, bf16[128,2048]{1,0:T(8,128)(2,1)S(1)}, u32[]{:S(2)}, u32[]{:S(2)}) collective-permute-start(bf16[128,2048]{1,0:T(8,128)(2,1)S(1)} %get-tuple-element.407), channel_id=1, source_target_pairs={{0,4},{1,5},{2,6},{3,7},{4,0},{5,1},{6,2},{7,3},{8,12},{9,13},{10,... | collective-permute-start | bytes 1572872 | tf_op jit(solution)/shard_map/ppermute | solution.py:57
  386.0 32.9 %collective-permute-start.30 = (bf16[128,2048]{1,0:T(8,128)(2,1)S(1)}, bf16[128,2048]{1,0:T(8,128)(2,1)S(1)}, u32[]{:S(2)}, u32[]{:S(2)}) collective-permute-start(bf16[128,2048]{1,0:T(8,128)(2,1)S(1)} %get-tuple-element.404), channel_id=1, source_target_pairs={{0,4},{1,5},{2,6},{3,7},{4,0},{5,1},{6,2},{7,3},{8,12},{9,13},{10,... | collective-permute-start | bytes 1572872 | tf_op jit(solution)/shard_map/ppermute | solution.py:57
  428.0 27.2 %collective-permute-start.48 = (bf16[256,2048]{1,0:T(8,128)(2,1)}, bf16[256,2048]{1,0:T(8,128)(2,1)}, u32[]{:S(2)}, u32[]{:S(2)}) collective-permute-start(bf16[256,2048]{1,0:T(8,128)(2,1)} %get-tuple-element.377), channel_id=1, source_target_pairs={{0,2},{1,3},{2,0},{3,1},{4,6},{5,7},{6,4},{7,5},{8,10},{9,11},{10,... | collective-permute-start | bytes 3145736 | tf_op jit(solution)/shard_map/ppermute | solution.py:57
  433.3 48.9 %collective-permute-start.52 = (bf16[256,2048]{1,0:T(8,128)(2,1)}, bf16[256,2048]{1,0:T(8,128)(2,1)}, u32[]{:S(2)}, u32[]{:S(2)}) collective-permute-start(bf16[256,2048]{1,0:T(8,128)(2,1)} %get-tuple-element.377), channel_id=1, source_target_pairs={{0,1},{1,0},{2,3},{3,2},{4,5},{5,4},{6,7},{7,6},{8,9},{9,8},{10,11... | collective-permute-start | bytes 3145736 | tf_op jit(solution)/shard_map/ppermute | solution.py:57
  472.3 222.4 %reduce-scatter.7.cloned.1.call-start = ((), (), s32[]{:S(2)}) async-start(), calls=%async_computation.9 | async-start | bytes 1310720 | tf_op jit(solution)/shard_map/reduce_scatter | solution.py:337
  618.3 93.1 %reduce-scatter.5.cloned.1.call-start = ((), (), s32[]{:S(2)}) async-start(), calls=%async_computation.8 | async-start | bytes 3932160 | tf_op jit(solution)/shard_map/reduce_scatter | solution.py:334
  652.0 33.8 %collective-permute-start.75 = (f32[1536]{0:T(1024)S(1)}, f32[1536]{0:T(1024)S(1)}, u32[]{:S(2)}, u32[]{:S(2)}) collective-permute-start(f32[1536]{0:T(1024)S(1)} %pad_maximum_fusion.3), channel_id=1, source_target_pairs={{0,16},{8,24},{16,0},{24,8},{1,17},{9,25},{17,1},{25,9},{2,18},{10... | collective-permute-start | bytes 18440 | tf_op jit(solution)/shard_map/ppermute | solution.py:107
  (126 other events, 1601.3 us)
Sparse Core Ops, SparseCore 0:
  10.2 66.1 all-gather.4
  78.0 26.6 all-gather.6
  106.2 80.1 all-gather.8
  187.8 79.2 all-gather.10
  338.7 74.6 reduce-scatter.10
  472.5 73.7 reduce-scatter.8
  618.5 24.0 reduce-scatter.6
  645.6 61.6 reduce-scatter.4

commit v2 on v1

v2 whole, which is shorter than its diff:
```python
import jax
import jax.numpy as jnp
from jax import lax
from jax.experimental import pallas as pl
from jax.experimental.pallas import tpu as pltpu
from jax.sharding import PartitionSpec as P

HEAD_DIM = 128


EPSILON = 1e-05
MASKED = -1e30


def layer_norm(values, gain_vec, bias_vec):
    row_mean = jnp.mean(values, axis=-1, keepdims=True)
    centred = values - row_mean
    variance = jnp.mean(centred * centred, axis=-1, keepdims=True)
    return centred * lax.rsqrt(variance + EPSILON) * gain_vec + bias_vec


def gelu_tanh(values):
    return jax.nn.gelu(values, approximate=True)


def contract_rows(left, right):
    return lax.dot_general(
        left, right, (((0,), (0,)), ((), ())), preferred_element_type=jnp.float32
    )


def contract_cols(left, right):
    return lax.dot_general(
        left, right, (((1,), (1,)), ((), ())), preferred_element_type=jnp.float32
    )


SWAP_TP = 8
BLOCK = 256
LOG2_E = 1.4426950408889634


def exchange(piece, mask):
    return lax.ppermute(piece, "tp", [(at, at ^ mask) for at in range(SWAP_TP)])


def gather_rows(piece):
    if lax.axis_size("tp") != SWAP_TP:
        return lax.all_gather(piece, "tp", axis=0, tiled=True)
    half = piece.shape[0] // 2
    from_x = exchange(piece, 2)
    from_y = exchange(piece, 4)
    own_twin = exchange(piece, 1)
    far_low = exchange(from_x[:half], 4)
    far_high = exchange(from_y[half:], 2)
    parts = [from_x, from_y, far_low, far_high]
    twins = [exchange(part, 1) for part in parts]
    return jnp.concatenate([piece, *parts, own_twin, *twins], axis=0)


def add_low(left, right):
    return (left.astype(jnp.float32) + right.astype(jnp.float32)).astype(jnp.bfloat16)


def scatter_rows(left, multiply):
    tp_count = lax.axis_size("tp")
    if tp_count != SWAP_TP:
        return lax.psum_scatter(multiply(left), "tp", scatter_dimension=0, tiled=True).astype(
            jnp.float32
        )
    rows = left.shape[0] // SWAP_TP
    half = rows // 2

    def both(first, count):
        twin = multiply(left[(4 + first) * rows : (4 + first + count) * rows])
        return add_low(multiply(left[first * rows : (first + count) * rows]), exchange(twin, 1))

    far = both(3, 1)
    far_low = exchange(far[:half], 2)
    far_high = exchange(far[half:], 4)
    mixed = both(1, 2)
    to_x, to_y = mixed[:rows], mixed[rows:]
    x_low = exchange(to_x[:half], 2)
    y_high = exchange(to_y[half:], 4)
    home = both(0, 1)
    x_high = exchange(add_low(to_x[half:], far_high), 2)
    y_low = exchange(add_low(to_y[:half], far_low), 4)
    wide = [part.astype(jnp.float32) for part in (x_low, x_high, y_low, y_high)]
    return (
        home.astype(jnp.float32)
        + jnp.concatenate(wide[:2], axis=0)
        + jnp.concatenate(wide[2:], axis=0)
    )


def sum_over(vector, axis):
    count = lax.axis_size(axis)
    terms = [vector] + [
        lax.ppermute(vector, axis, [(at, at ^ step) for at in range(count)])
        for step in range(1, count)
    ]
    while len(terms) > 1:
        terms = [terms[at] + terms[at + 1] for at in range(0, len(terms), 2)]
    return terms[0]


def block_table(seq_len, seq_group, group_id, block_count):
    seq_order = jnp.arange(seq_len.shape[0], dtype=jnp.int32)
    same_before = (seq_group[None, :] == seq_group[:, None]) & (
        seq_order[None, :] < seq_order[:, None]
    )
    starts = jnp.sum(jnp.where(same_before, seq_len[None, :], 0), axis=1) // BLOCK
    ends = starts + seq_len // BLOCK
    block_at = jnp.arange(block_count, dtype=jnp.int32)
    inside = (
        (seq_group[None, :] == group_id)
        & (starts[None, :] <= block_at[:, None])
        & (block_at[:, None] < ends[None, :])
    )
    held = jnp.sum(inside.astype(jnp.int32), axis=1)
    first = jnp.sum(jnp.where(inside, starts[None, :], 0), axis=1)
    first = jnp.where(held > 0, first, block_at)
    place = block_at
    if lax.axis_size("tp") == SWAP_TP:
        apart = block_at ^ lax.axis_index("tp")
        place = (apart >> 1) + 4 * (apart & 1)
    return jnp.stack([place, first, held]).astype(jnp.int32)


def dot_nt(left, right):
    return lax.dot_general(
        left, right, (((1,), (1,)), ((), ())), preferred_element_type=jnp.float32
    )


def block_rows(place):
    return pl.ds(pl.multiple_of(place * BLOCK, BLOCK), BLOCK)


def attend_kernel(table, qkv, ctx, lse):
    head_cols = ctx.shape[1]
    heads = head_cols // HEAD_DIM
    sharpness = HEAD_DIM ** (-0.5) * LOG2_E
    row_at = lax.broadcasted_iota(jnp.int32, (BLOCK, BLOCK), 0)
    col_at = lax.broadcasted_iota(jnp.int32, (BLOCK, BLOCK), 1)

    def cols(part, head):
        return pl.ds(part * head_cols + head * HEAD_DIM, HEAD_DIM)

    def query_block(at, _):
        rows = block_rows(table[0, at])
        queries = [qkv[rows, cols(0, head)] for head in range(heads)]
        allowed = (col_at == row_at) | ((col_at < row_at) & (table[2, at] > 0))

        def start(head):
            scores = dot_nt(queries[head], qkv[rows, cols(1, head)]) * sharpness
            scores = jnp.where(allowed, scores, MASKED)
            top = jnp.max(scores, axis=-1, keepdims=True)
            weights = jnp.exp2(scores - top)
            total = jnp.sum(weights, axis=-1, keepdims=True)
            mixed = jnp.dot(
                weights.astype(jnp.bfloat16),
                qkv[rows, cols(2, head)],
                preferred_element_type=jnp.float32,
            )
            return top, total, mixed

        def key_block(key_at, carried):
            key_rows = block_rows(table[0, key_at])
            result = []
            for head in range(heads):
                top, total, mixed = carried[head]
                scores = dot_nt(queries[head], qkv[key_rows, cols(1, head)]) * sharpness
                new_top = jnp.maximum(top, jnp.max(scores, axis=-1, keepdims=True))
                shrink = jnp.exp2(top - new_top)
                weights = jnp.exp2(scores - new_top)
                total = total * shrink + jnp.sum(weights, axis=-1, keepdims=True)
                mixed = mixed * shrink + jnp.dot(
                    weights.astype(jnp.bfloat16),
                    qkv[key_rows, cols(2, head)],
                    preferred_element_type=jnp.float32,
                )
                result.append((new_top, total, mixed))
            return tuple(result)

        done = lax.fori_loop(
            table[1, at], at, key_block, tuple(start(head) for head in range(heads))
        )
        for head in range(heads):
            top, total, mixed = done[head]
            ctx[rows, pl.ds(head * HEAD_DIM, HEAD_DIM)] = (mixed / total).astype(jnp.bfloat16)
            level = jnp.broadcast_to(top + jnp.log2(total), (BLOCK, HEAD_DIM))
            lse[pl.ds(head * 8, 8), rows] = level.T[:8]
        return 0

    lax.fori_loop(0, table.shape[1], query_block, 0)


def attend_back_kernel(table, qkv, ctx, ctx_grad, lse, qkv_grad, sums, key_acc, value_acc):
    head_cols = ctx.shape[1]
    heads = head_cols // HEAD_DIM
    scaling = HEAD_DIM ** (-0.5)
    sharpness = scaling * LOG2_E
    key_row = lax.broadcasted_iota(jnp.int32, (BLOCK, BLOCK), 0)
    query_col = lax.broadcasted_iota(jnp.int32, (BLOCK, BLOCK), 1)
    sums[...] = jnp.zeros_like(sums)

    def cols(part, head):
        return pl.ds(part * head_cols + head * HEAD_DIM, HEAD_DIM)

    def query_block(at, _):
        rows = block_rows(table[0, at])
        queries, grads, levels, dots = [], [], [], []
        for head in range(heads):
            own = pl.ds(head * HEAD_DIM, HEAD_DIM)
            queries.append(qkv[rows, cols(0, head)])
            grads.append(ctx_grad[rows, own])
            levels.append(lse[pl.ds(head * 8, 1), rows])
            dot = jnp.sum(
                grads[head].astype(jnp.float32) * ctx[rows, own].astype(jnp.float32),
                axis=-1,
                keepdims=True,
            )
            dots.append(jnp.broadcast_to(dot, (BLOCK, HEAD_DIM)).T[:1])
        allowed = (key_row == query_col) | ((key_row < query_col) & (table[2, at] > 0))

        def tile(head, key_rows, masked):
            keys = qkv[key_rows, cols(1, head)]
            probs = jnp.exp2(dot_nt(keys, queries[head]) * sharpness - levels[head])
            if masked:
                probs = jnp.where(allowed, probs, 0.0)
            prob_grad = dot_nt(qkv[key_rows, cols(2, head)], grads[head])
            score_grad = (probs * (prob_grad - dots[head])).astype(jnp.bfloat16)
            value_part = jnp.dot(
                probs.astype(jnp.bfloat16), grads[head], preferred_element_type=jnp.float32
            )
            key_part = jnp.dot(score_grad, queries[head], preferred_element_type=jnp.float32)
            return contract_rows(score_grad, keys), key_part, value_part

        query_acc = []
        for head in range(heads):
            own = pl.ds(head * HEAD_DIM, HEAD_DIM)
            query_part, key_part, value_part = tile(head, rows, True)
            key_acc[rows, own] = key_part
            value_acc[rows, own] = value_part
            query_acc.append(query_part)

        def key_block(key_at, carried):
            key_rows = block_rows(table[0, key_at])
            result = []
            for head in range(heads):
                own = pl.ds(head * HEAD_DIM, HEAD_DIM)
                query_part, key_part, value_part = tile(head, key_rows, False)
                key_acc[key_rows, own] += key_part
                value_acc[key_rows, own] += value_part
                result.append(carried[head] + query_part)
            return tuple(result)

        query_acc = lax.fori_loop(table[1, at], at, key_block, tuple(query_acc))
        for head in range(heads):
            low = (query_acc[head] * scaling).astype(jnp.bfloat16)
            qkv_grad[rows, cols(0, head)] = low
            sums[:1, pl.ds(head * HEAD_DIM, HEAD_DIM)] += jnp.sum(
                low.astype(jnp.float32), axis=0, keepdims=True
            )
        return 0

    lax.fori_loop(0, table.shape[1], query_block, 0)

    def finish(at, _):
        rows = block_rows(at)
        key_low = (key_acc[rows, :] * scaling).astype(jnp.bfloat16)
        value_low = value_acc[rows, :].astype(jnp.bfloat16)
        qkv_grad[rows, pl.ds(head_cols, head_cols)] = key_low
        qkv_grad[rows, pl.ds(2 * head_cols, head_cols)] = value_low
        sums[1:2, :] += jnp.sum(value_low.astype(jnp.float32), axis=0, keepdims=True)
        return 0

    lax.fori_loop(0, table.shape[1], finish, 0)


def whole_specs(count):
    return [pl.BlockSpec(memory_space=pltpu.VMEM) for _ in range(count)]


def attend(table, qkv_rows, head_cols):
    rows = qkv_rows.shape[0]
    heads = head_cols // HEAD_DIM
    return pl.pallas_call(
        attend_kernel,
        out_shape=(
            jax.ShapeDtypeStruct((rows, head_cols), jnp.bfloat16),
            jax.ShapeDtypeStruct((8 * heads, rows), jnp.float32),
        ),
        in_specs=[pl.BlockSpec(memory_space=pltpu.SMEM), *whole_specs(1)],
        out_specs=tuple(whole_specs(2)),
        name="attend",
    )(table, qkv_rows)


def attend_back(table, qkv_rows, context, ctx_grad, lse):
    rows, head_cols = context.shape
    return pl.pallas_call(
        attend_back_kernel,
        out_shape=(
            jax.ShapeDtypeStruct(qkv_rows.shape, jnp.bfloat16),
            jax.ShapeDtypeStruct((8, head_cols), jnp.float32),
        ),
        in_specs=[pl.BlockSpec(memory_space=pltpu.SMEM), *whole_specs(4)],
        out_specs=tuple(whole_specs(2)),
        scratch_shapes=[
            pltpu.VMEM((rows, head_cols), jnp.float32),
            pltpu.VMEM((rows, head_cols), jnp.float32),
        ],
        name="attend_back",
    )(table, qkv_rows, context, ctx_grad, lse)


def local(
    tokens,
    seq_len,
    seq_group,
    ln1_gain,
    ln1_bias,
    qkv_weight,
    qv_bias,
    out_weight,
    out_bias,
    ln2_gain,
    ln2_bias,
    up_weight,
    up_bias,
    down_weight,
    down_bias,
    out_grad,
):
    width = tokens.shape[1]
    head_cols = qkv_weight.shape[2]
    table = block_table(
        seq_len,
        seq_group,
        lax.axis_index("fsdp"),
        tokens.shape[0] * lax.axis_size("tp") // BLOCK,
    )

    def gather_weights():
        return (
            lax.all_gather(qkv_weight, "fsdp", axis=0, tiled=True),
            lax.all_gather(out_weight, "fsdp", axis=1, tiled=True),
            lax.all_gather(up_weight, "fsdp", axis=0, tiled=True),
            lax.all_gather(down_weight, "fsdp", axis=1, tiled=True),
        )

    inputs = tokens.astype(jnp.float32)
    norm1 = layer_norm(inputs, ln1_gain, ln1_bias).astype(jnp.bfloat16)
    qkv_full, out_full, up_full, down_full = gather_weights()
    qkv_flat = qkv_full.reshape(width, 3 * head_cols)
    qkv_shift = jnp.concatenate([qv_bias[0], jnp.zeros_like(qv_bias[0]), qv_bias[1]])
    norm1_rows = gather_rows(norm1)
    qkv_rows = (
        jnp.dot(
            norm1_rows,
            qkv_flat,
            preferred_element_type=jnp.float32,
        )
        + qkv_shift
    ).astype(jnp.bfloat16)
    out_grad, norm1_rows = lax.optimization_barrier((out_grad, norm1_rows))
    grad_piece = gather_rows(out_grad)
    context, lse = attend(table, qkv_rows, head_cols)
    context, grad_piece = lax.optimization_barrier((context, grad_piece))
    attn_rows = scatter_rows(
        context,
        lambda part: jnp.dot(part, out_full, preferred_element_type=jnp.float32).astype(
            jnp.bfloat16
        ),
    )
    middle = inputs + attn_rows + out_bias
    norm2 = layer_norm(middle, ln2_gain, ln2_bias).astype(jnp.bfloat16)
    norm_piece = gather_rows(norm2)
    pre = (
        jnp.dot(
            norm_piece,
            up_full,
            preferred_element_type=jnp.float32,
        )
        + up_bias
    )
    act_rows = gelu_tanh(pre).astype(jnp.bfloat16)
    mlp_rows = scatter_rows(
        act_rows,
        lambda part: jnp.dot(part, down_full, preferred_element_type=jnp.float32).astype(
            jnp.bfloat16
        ),
    )
    layer_out = (middle + mlp_rows + down_bias).astype(jnp.bfloat16)
    grad_rows = out_grad.astype(jnp.float32)
    act_value, gelu_back = jax.vjp(gelu_tanh, pre)
    act_piece = act_value.astype(jnp.bfloat16)
    down_acc = contract_rows(act_piece, grad_piece)
    act_grad = contract_cols(grad_piece, down_full)
    pre_grad = gelu_back(act_grad)[0].astype(jnp.bfloat16)
    up_acc = contract_rows(norm_piece, pre_grad)
    shift_acc = jnp.sum(pre_grad.astype(jnp.float32), axis=0)
    norm2_grad = scatter_rows(
        pre_grad, lambda part: contract_cols(part, up_full).astype(jnp.bfloat16)
    )
    unused_two, ln2_back = jax.vjp(layer_norm, middle, ln2_gain, ln2_bias)
    middle_ln, grad_g2, grad_b2 = ln2_back(norm2_grad)
    middle_grad = grad_rows + middle_ln
    proj_grad = middle_grad.astype(jnp.bfloat16)
    portion = gather_rows(proj_grad)
    out_acc = contract_rows(context, portion)
    ctx_grad = contract_cols(portion, out_full).astype(jnp.bfloat16)
    grad_out_w = out_acc
    qkv_grad, sums = attend_back(table, qkv_rows, context, ctx_grad, lse)
    early = sum_over(
        sum_over(
            jnp.stack([jnp.sum(middle_grad, axis=0), grad_g2, grad_b2, jnp.sum(grad_rows, axis=0)]),
            "fsdp",
        ),
        "tp",
    )
    qkv_grad, early = lax.optimization_barrier((qkv_grad, early))
    qv_sums = sums[:2]
    norm1_grad = scatter_rows(
        qkv_grad, lambda part: contract_cols(part, qkv_flat).astype(jnp.bfloat16)
    )
    unused_one, ln1_back = jax.vjp(layer_norm, inputs, ln1_gain, ln1_bias)
    input_ln, grad_g1, grad_b1 = ln1_back(norm1_grad)
    tokens_grad = (middle_grad + input_ln).astype(jnp.bfloat16)
    grad_qkv_flat = contract_rows(norm1_rows, qkv_grad)
    grad_qkv_w = grad_qkv_flat.reshape(width, 3, head_cols)
    shard_qkv, shard_out, shard_up, shard_down = (
        lax.psum_scatter(
            grad_qkv_w.astype(jnp.bfloat16), "fsdp", scatter_dimension=0, tiled=True
        ).astype(jnp.float32),
        lax.psum_scatter(
            grad_out_w.astype(jnp.bfloat16), "fsdp", scatter_dimension=1, tiled=True
        ).astype(jnp.float32),
        lax.psum_scatter(
            up_acc.astype(jnp.bfloat16), "fsdp", scatter_dimension=0, tiled=True
        ).astype(jnp.float32),
        lax.psum_scatter(
            down_acc.astype(jnp.bfloat16), "fsdp", scatter_dimension=1, tiled=True
        ).astype(jnp.float32),
    )
    own_sums = sum_over(jnp.concatenate([qv_sums.reshape(-1), shift_acc]), "fsdp")
    grad_qv = own_sums[: 2 * head_cols].reshape(2, head_cols)
    grad_upb_own = own_sums[2 * head_cols :]
    late = sum_over(sum_over(jnp.stack([grad_g1, grad_b1]), "fsdp"), "tp")
    return (
        layer_out,
        tokens_grad,
        late[0],
        late[1],
        shard_qkv,
        grad_qv,
        shard_out,
        early[0],
        early[1],
        early[2],
        shard_up,
        grad_upb_own,
        shard_down,
        early[3],
    )


def solution(mesh):
    placed = (
        P(("fsdp", "tp"), None),
        P(),
        P(),
        P(),
        P(),
        P("fsdp", None, "tp"),
        P(None, "tp"),
        P("tp", "fsdp"),
        P(),
        P(),
        P(),
        P("fsdp", "tp"),
        P("tp"),
        P("tp", "fsdp"),
        P(),
        P(("fsdp", "tp"), None),
    )
    return jax.shard_map(
        local,
        mesh=mesh,
        in_specs=placed,
        out_specs=(
            P(("fsdp", "tp"), None),
            P(("fsdp", "tp"), None),
            P(),
            P(),
            P("fsdp", None, "tp"),
            P(None, "tp"),
            P("tp", "fsdp"),
            P(),
            P(),
            P(),
            P("fsdp", "tp"),
            P("tp"),
            P("tp", "fsdp"),
            P(),
        ),
        check_vma=False,
    )
```

time: 733 us -> 655 us (0.89)
  local copies, waits for them, and re-layouts: 121 us -> 51.2 us
  waiting for transfers between devices: 194 us -> 263 us
  matrix products: 221 us -> 160 us
  Pallas kernels: 0 us -> 54.5 us
  other arithmetic: 71 us -> 25.3 us
  loops' own time: 13.6 us -> 0 us
  between operations: 25.9 us -> 15.4 us
    dot_general x32 -> x12, matrix products: 98.3 us -> 34.9 us  [the longest x6 25.6 us: local(): jnp.dot(part, down_full, preferred_element_type=jnp.float32)]
    pallas_call x0 -> x2, Pallas kernels: none -> 54.5 us  [the longest x1 28.6 us: attend_back(): pl.pallas_call(attend_back_kernel, out_shape=(jax.ShapeDtypeStruct(qkv_ro...]
    ppermute x64 -> x72, waiting for transfers between devices: 183 us -> 237 us  [exchange(): return lax.ppermute(piece, 'tp', [(at, at ^ mask) for at in range(SWAP_TP)])]
    unnamed x160 -> x116, local copies, waits for them, and re-layouts: 71.6 us -> 37.4 us
    another operation x2 -> x0, loops' own time: 13.6 us -> none  [the longest x1 10.6 us: local(): lax.scan(attend_back, acc_start, jnp.arange(blk_count))]
    reduce_scatter x1, waiting for transfers between devices: 0.01 us -> 13.2 us  [local(): lax.psum_scatter(grad_qkv_w.astype(jnp.bfloat16), 'fsdp', scatter_dimensi...]
    reduce_sum x8 -> x2, other arithmetic: 12.6 us -> 0.33 us  [the longest x1 0.18 us: block_table(): jnp.sum(jnp.where(same_before, seq_len[None, :], 0), axis=1) // BLOCK]
    dynamic_slice x28 -> x0, local copies, waits for them, and re-layouts: 10.4 us -> none  [the longest x8 4.67 us: local(): ctx_blocks, lse_blocks = lax.map(attend_block, jnp.arange(blk_count))]
  transfers between devices with their start and end apart: 95 -> 103, of which waited for: 29 -> 45; matrix products, arithmetic and copies ran while one was open for 51% -> 30% of each run, Pallas kernels for 0% -> 8%
where the time goes in v2:
time: 655 us; the launch traced here: 645 us
  waiting for transfers between devices  263 us (40%)
  matrix products  160 us (24%)
  starting transfers between devices  75.9 us (12%)
  Pallas kernels  54.5 us (8%)
  local copies, waits for them, and re-layouts  51.2 us (8%)
  other arithmetic  25.3 us (4%)
  between operations  15.4 us (2%)
    ppermute x72, waiting for transfers between devices, exchange(): return lax.ppermute(piece, 'tp', [(at, at ^ mask) for at in range(SWAP_TP)])  237 us
    dot_general x14, matrix products, contract_cols(): lax.dot_general(left, right, (((1,), (1,)), ((), ())), preferred_element_...  57.7 us
    ppermute x72, starting transfers between devices, exchange(): return lax.ppermute(piece, 'tp', [(at, at ^ mask) for at in range(SWAP_TP)])  54.4 us
    dot_general x4, matrix products, contract_rows(): lax.dot_general(left, right, (((0,), (0,)), ((), ())), preferred_element_...  41.2 us
    unnamed x116, local copies, waits for them, and re-layouts  37.4 us
    pallas_call x1, Pallas kernels, attend_back(): pl.pallas_call(attend_back_kernel, out_shape=(jax.ShapeDtypeStruct(qkv_ro...  28.6 us
    pallas_call x1, Pallas kernels, attend(): pl.pallas_call(attend_kernel, out_shape=(jax.ShapeDtypeStruct((rows, head...  25.9 us
    dot_general x6, matrix products, local(): jnp.dot(part, down_full, preferred_element_type=jnp.float32)  25.6 us
  transfers between devices with their start and end apart: 103, of which 45 were waited for; matrix products, arithmetic and copies ran while one was open for 30% of the time, Pallas kernels for 8%

profile of v2, /device:TPU:0, one launch (start us, length us, event | category | flops | bytes accessed | tf_op | source)
XLA Modules:
  0.0 645.3 jit_solution(17715138331631851669)
XLA Ops:
  18.8 21.8 %collective-permute-done.1 = bf16[256,2048]{1,0:T(8,128)(2,1)S(1)} collective-permute-done((bf16[256,2048]{1,0:T(8,128)(2,1)}, bf16[256,2048]{1,0:T(8,128)(2,1)S(1)}, u32[]{:S(2)}, u32[]{:S(2)}) %collective-permute-start.1) | collective-permute-done | bytes 1048608 | tf_op jit(solution)/shard_map/ppermute | solution.py:44
  67.3 22.4 %collective-permute-done.10 = bf16[256,2048]{1,0:T(8,128)(2,1)S(1)} collective-permute-done((bf16[256,2048]{1,0:T(8,128)(2,1)S(1)}, bf16[256,2048]{1,0:T(8,128)(2,1)S(1)}, u32[]{:S(2)}, u32[]{:S(2)}) %collective-permute-start.10) | collective-permute-done | bytes 1048608 | tf_op jit(solution)/shard_map/ppermute | solution.py:44
  111.9 11.8 %add_convert_fusion.qkv = bf16[2048,768]{1,0:T(8,128)(2,1)} fusion(f32[768]{0:T(1024)S(1)} %pad_maximum_fusion.3, bf16[2048,2048]{1,0:T(8,128)(2,1)} %constant_dynamic-update-slice_fusion, bf16[2048,768]{0,1:T(8,128)(2,1)} %bitcast.89), kind=kOutput, calls=%fused_computation.11 | convolution fusion | flops 6445596672 | bytes 14683136 | tf_op jit(solution)/shard_map/dot_general | solution.py:361
  123.7 25.9 %attend.1 = (bf16[2048,256]{1,0:T(8,128)(2,1)}, f32[16,2048]{1,0:T(8,128)}) custom-call(s32[3,8]{1,0:T(4,128)} %pad_add_fusion.table, bf16[2048,768]{1,0:T(8,128)(2,1)} %add_convert_fusion.qkv), custom_call_target="tpu_custom_call" | custom-call | tf_op jit(solution)/shard_map/attend/pallas_call | solution.py:289
  159.6 9.6 %collective-permute-done.24 = bf16[128,2048]{1,0:T(8,128)(2,1)S(1)} collective-permute-done((bf16[128,2048]{1,0:T(8,128)(2,1)S(1)}, bf16[128,2048]{1,0:T(8,128)(2,1)S(1)}, u32[]{:S(2)}, u32[]{:S(2)}) %collective-permute-start.24) | collective-permute-done | bytes 524320 | tf_op jit(solution)/shard_map/ppermute | solution.py:44
  176.8 9.6 %collective-permute-done.25 = bf16[128,2048]{1,0:T(8,128)(2,1)} collective-permute-done((bf16[128,2048]{1,0:T(8,128)(2,1)}, bf16[128,2048]{1,0:T(8,128)(2,1)}, u32[]{:S(2)}, u32[]{:S(2)}) %collective-permute-start.25) | collective-permute-done | bytes 524320 | tf_op jit(solution)/shard_map/ppermute | solution.py:44
  187.8 8.1 %collective-permute-done.26 = bf16[128,2048]{1,0:T(8,128)(2,1)} collective-permute-done((bf16[128,2048]{1,0:T(8,128)(2,1)}, bf16[128,2048]{1,0:T(8,128)(2,1)}, u32[]{:S(2)}, u32[]{:S(2)}) %collective-permute-start.26) | collective-permute-done | bytes 524320 | tf_op jit(solution)/shard_map/ppermute | solution.py:44
  203.7 21.7 %collective-permute-done.28 = bf16[256,2048]{1,0:T(8,128)(2,1)S(1)} collective-permute-done((bf16[256,2048]{1,0:T(8,128)(2,1)S(1)}, bf16[256,2048]{1,0:T(8,128)(2,1)S(1)}, u32[]{:S(2)}, u32[]{:S(2)}) %collective-permute-start.28) | collective-permute-done | bytes 1048608 | tf_op jit(solution)/shard_map/ppermute | solution.py:44
  244.3 14.5 %fusion.92 = f32[2048,1024]{1,0:T(8,128)} fusion(bf16[2048,2048]{1,0:T(8,128)(2,1)} %constant_dynamic-update-slice_fusion.20, bf16[2048,1024]{1,0:T(8,128)(2,1)} %all-gather.9.cloned.1.call-done), kind=kOutput, calls=%fused_computation.218 | convolution fusion | flops 8589934592 | bytes 20971520 | tf_op jit(solution)/shard_map/dot_general | solution.py:382
  258.8 8.2 %all-gather.11.cloned.1.call-done = bf16[1024,2048]{1,0:T(8,128)(2,1)} async-done(((bf16[1024,512]{1,0:T(8,128)(2,1)}), bf16[1024,2048]{1,0:T(8,128)(2,1)}) %all-gather.11.cloned.1.call-update) | async-done | bytes 4194320 | tf_op jit(solution)/shard_map/all_gather | solution.py:351
  267.0 20.6 %convert_reduce_fusion = (f32[1024]{0:T(1024)S(1)}, bf16[2048,1024]{1,0:T(8,128)(2,1)S(1)}, bf16[2048,1024]{1,0:T(8,128)(2,1)}) fusion(f32[2048,1024]{1,0:T(8,128)} %fusion.92, f32[1024]{0:T(1024)S(1)} %copy-done.35, bf16[2048,2048]{1,0:T(8,128)(2,1)} %constant_dynamic-update-slice_fusion.10, bf16[1024,2048]{1,0:T(8,128)(2,1)} %all-gather.11.cloned.1.call-done), kind=kOutput, calls=%fused_computation.9 | convolution fusion | flops 8642362368 | bytes 29368320 | tf_op jit(solution)/shard_map/dot_general | solution.py:33
  302.6 8.6 %collective-permute-done.51 = bf16[128,2048]{1,0:T(8,128)(2,1)S(1)} collective-permute-done((bf16[128,2048]{1,0:T(8,128)(2,1)S(1)}, bf16[128,2048]{1,0:T(8,128)(2,1)S(1)}, u32[]{:S(2)}, u32[]{:S(2)}) %collective-permute-start.51) | collective-permute-done | bytes 524320 | tf_op jit(solution)/shard_map/ppermute | solution.py:44
  317.0 10.6 %collective-permute-done.52 = bf16[128,2048]{1,0:T(8,128)(2,1)S(1)} collective-permute-done((bf16[128,2048]{1,0:T(8,128)(2,1)S(1)}, bf16[128,2048]{1,0:T(8,128)(2,1)S(1)}, u32[]{:S(2)}, u32[]{:S(2)}) %collective-permute-start.52) | collective-permute-done | bytes 524320 | tf_op jit(solution)/shard_map/ppermute | solution.py:44
  344.1 21.8 %collective-permute-done.55 = bf16[256,2048]{1,0:T(8,128)(2,1)S(1)} collective-permute-done((bf16[256,2048]{1,0:T(8,128)(2,1)S(1)}, bf16[256,2048]{1,0:T(8,128)(2,1)S(1)}, u32[]{:S(2)}, u32[]{:S(2)}) %collective-permute-start.55) | collective-permute-done | bytes 1048608 | tf_op jit(solution)/shard_map/ppermute | solution.py:44
  387.0 14.1 %convolution_convert_fusion = bf16[1024,2048]{1,0:T(8,128)(2,1)} fusion(bf16[2048,1024]{1,0:T(8,128)(2,1)} %get-tuple-element.56, bf16[2048,2048]{1,0:T(8,128)(2,1)} %constant_dynamic-update-slice_fusion.10), kind=kOutput, calls=%fused_computation.16 | convolution fusion | flops 8592031744 | bytes 16777216 | tf_op jit(solution)/shard_map/dot_general | solution.py:27
  415.0 13.2 %convolution_convert_fusion.1 = bf16[2048,1024]{1,0:T(8,128)(2,1)} fusion(bf16[2048,2048]{1,0:T(8,128)(2,1)} %constant_dynamic-update-slice_fusion.20, bf16[2048,1024]{1,0:T(8,128)(2,1)S(1)} %copy-done.37), kind=kOutput, calls=%fused_computation.17 | convolution fusion | flops 8592031744 | bytes 16777216 | tf_op jit(solution)/shard_map/dot_general | solution.py:27
  438.9 7.9 %collective-permute-done.42 = bf16[128,2048]{1,0:T(8,128)(2,1)S(1)} collective-permute-done((bf16[128,2048]{1,0:T(8,128)(2,1)S(1)}, bf16[128,2048]{1,0:T(8,128)(2,1)S(1)}, u32[]{:S(2)}, u32[]{:S(2)}) %collective-permute-start.42) | collective-permute-done | bytes 524320 | tf_op jit(solution)/shard_map/ppermute | solution.py:44
  473.4 8.7 %collective-permute-done.38 = bf16[128,2048]{1,0:T(8,128)(2,1)S(1)} collective-permute-done((bf16[128,2048]{1,0:T(8,128)(2,1)S(1)}, bf16[128,2048]{1,0:T(8,128)(2,1)S(1)}, u32[]{:S(2)}, u32[]{:S(2)}) %collective-permute-start.38) | collective-permute-done | bytes 524320 | tf_op jit(solution)/shard_map/ppermute | solution.py:44
  492.5 28.6 %attend_back.1 = (bf16[2048,768]{1,0:T(8,128)(2,1)}, f32[8,256]{1,0:T(8,128)}) custom-call(s32[3,8]{1,0:T(4,128)} %pad_add_fusion.table, bf16[2048,768]{1,0:T(8,128)(2,1)} %add_convert_fusion.qkv, bf16[2048,256]{1,0:T(8,128)(2,1)} %get-tuple-element.26.ctx, bf16[2048,256]{1,0:T(8,128)(2,1)} %convolution_convert_fusion.28.ctx_grad, ...), custom_call_target="tpu_custom_call" | custom-call | tf_op jit(solution)/shard_map/attend_back/pallas_call | solution.py:303
  529.3 10.6 %convolution_convert_fusion.2 = bf16[2048,768]{0,1:T(8,128)(2,1)} fusion(bf16[2048,2048]{1,0:T(8,128)(2,1)} %constant_dynamic-update-slice_fusion, bf16[2048,768]{1,0:T(8,128)(2,1)S(1)} %copy-done.32), kind=kOutput, calls=%fused_computation.18 | convolution fusion | flops 6444023808 | bytes 14680064 | tf_op jit(solution)/shard_map/dot_general | solution.py:27
  559.1 8.4 %collective-permute-done.79 = bf16[128,2048]{1,0:T(8,128)(2,1)S(1)} collective-permute-done((bf16[128,2048]{1,0:T(8,128)(2,1)S(1)}, bf16[128,2048]{1,0:T(8,128)(2,1)S(1)}, u32[]{:S(2)}, u32[]{:S(2)}) %collective-permute-start.79) | collective-permute-done | bytes 524320 | tf_op jit(solution)/shard_map/ppermute | solution.py:44
  573.1 9.9 %collective-permute-done.80 = bf16[128,2048]{1,0:T(8,128)(2,1)S(1)} collective-permute-done((bf16[128,2048]{1,0:T(8,128)(2,1)S(1)}, bf16[128,2048]{1,0:T(8,128)(2,1)S(1)}, u32[]{:S(2)}, u32[]{:S(2)}) %collective-permute-start.80) | collective-permute-done | bytes 524320 | tf_op jit(solution)/shard_map/ppermute | solution.py:44
  584.7 8.1 %collective-permute-done.81 = bf16[128,2048]{1,0:T(8,128)(2,1)S(1)} collective-permute-done((bf16[128,2048]{1,0:T(8,128)(2,1)S(1)}, bf16[128,2048]{1,0:T(8,128)(2,1)S(1)}, u32[]{:S(2)}, u32[]{:S(2)}) %collective-permute-start.81) | collective-permute-done | bytes 524320 | tf_op jit(solution)/shard_map/ppermute | solution.py:44
  622.7 13.2 %reduce-scatter.5.cloned.1.call-done = bf16[512,3,256]{2,0,1:T(8,128)(2,1)} async-done(((bf16[2048,3,256]{2,0,1:T(8,128)(2,1)}), bf16[512,3,256]{2,0,1:T(8,128)(2,1)}) %reduce-scatter.5.cloned.1.call-update) | async-done | bytes 786448 | tf_op jit(solution)/shard_map/reduce_scatter | solution.py:435
  (410 shorter events, 292.1 us)
Async XLA Ops:
  7.2 104.7 %all-gather.5.cloned.1.call-start = ((), (), s32[]{:S(2)}) async-start(), calls=%async_computation.4 | async-start | bytes 3932160 | tf_op jit(solution)/shard_map/all_gather | solution.py:348
  9.7 140.0 %all-gather.7.cloned.1.call-start = ((), (), s32[]{:S(2)}) async-start(), calls=%async_computation.5 | async-start | bytes 1310720 | tf_op jit(solution)/shard_map/all_gather | solution.py:349
  10.4 233.8 %all-gather.9.cloned.1.call-start = ((), (), s32[]{:S(2)}) async-start(), calls=%async_computation.6 | async-start | bytes 5242880 | tf_op jit(solution)/shard_map/all_gather | solution.py:350
  14.2 26.4 %collective-permute-start.1 = (bf16[256,2048]{1,0:T(8,128)(2,1)}, bf16[256,2048]{1,0:T(8,128)(2,1)S(1)}, u32[]{:S(2)}, u32[]{:S(2)}) collective-permute-start(bf16[256,2048]{1,0:T(8,128)(2,1)} %get-tuple-element.53), channel_id=1, source_target_pairs={{0,4},{1,5},{2,6},{3,7},{4,0},{5,1},{6,2},{7,3},{8,12},{9,13},{10,... | collective-permute-start | bytes 3145736 | tf_op jit(solution)/shard_map/ppermute | solution.py:44
  17.2 25.2 %collective-permute-start = (bf16[256,2048]{1,0:T(8,128)(2,1)}, bf16[256,2048]{1,0:T(8,128)(2,1)}, u32[]{:S(2)}, u32[]{:S(2)}) collective-permute-start(bf16[256,2048]{1,0:T(8,128)(2,1)} %get-tuple-element.53), channel_id=1, source_target_pairs={{0,2},{1,3},{2,0},{3,1},{4,6},{5,7},{6,4},{7,5},{8,10},{9,11},{10,... | collective-permute-start | bytes 3145736 | tf_op jit(solution)/shard_map/ppermute | solution.py:44
  18.7 39.2 %collective-permute-start.4 = (bf16[256,2048]{1,0:T(8,128)(2,1)}, bf16[256,2048]{1,0:T(8,128)(2,1)}, u32[]{:S(2)}, u32[]{:S(2)}) collective-permute-start(bf16[256,2048]{1,0:T(8,128)(2,1)} %get-tuple-element.53), channel_id=1, source_target_pairs={{0,1},{1,0},{2,3},{3,2},{4,5},{5,4},{6,7},{7,6},{8,9},{9,8},{10,11... | collective-permute-start | bytes 3145736 | tf_op jit(solution)/shard_map/ppermute | solution.py:44
  18.7 248.3 %all-gather.11.cloned.1.call-start = ((), (), s32[]{:S(2)}) async-start(), calls=%async_computation.7 | async-start | bytes 5242880 | tf_op jit(solution)/shard_map/all_gather | solution.py:351
  64.1 25.6 %collective-permute-start.10 = (bf16[256,2048]{1,0:T(8,128)(2,1)S(1)}, bf16[256,2048]{1,0:T(8,128)(2,1)S(1)}, u32[]{:S(2)}, u32[]{:S(2)}) collective-permute-start(bf16[256,2048]{1,0:T(8,128)(2,1)S(1)} %copy-done.7), channel_id=1, source_target_pairs={{0,4},{1,5},{2,6},{3,7},{4,0},{5,1},{6,2},{7,3},{8,12},{9,13},{10,... | collective-permute-start | bytes 3145736 | tf_op jit(solution)/shard_map/ppermute | solution.py:44
  65.6 25.4 %collective-permute-start.9 = (bf16[256,2048]{1,0:T(8,128)(2,1)S(1)}, bf16[256,2048]{1,0:T(8,128)(2,1)}, u32[]{:S(2)}, u32[]{:S(2)}) collective-permute-start(bf16[256,2048]{1,0:T(8,128)(2,1)S(1)} %copy-done.7), channel_id=1, source_target_pairs={{0,2},{1,3},{2,0},{3,1},{4,6},{5,7},{6,4},{7,5},{8,10},{9,11},{10,... | collective-permute-start | bytes 3145736 | tf_op jit(solution)/shard_map/ppermute | solution.py:44
  67.2 39.9 %collective-permute-start.13 = (bf16[256,2048]{1,0:T(8,128)(2,1)S(1)}, bf16[256,2048]{1,0:T(8,128)(2,1)S(1)}, u32[]{:S(2)}, u32[]{:S(2)}) collective-permute-start(bf16[256,2048]{1,0:T(8,128)(2,1)S(1)} %copy-done.7), channel_id=1, source_target_pairs={{0,1},{1,0},{2,3},{3,2},{4,5},{5,4},{6,7},{7,6},{8,9},{9,8},{10,11... | collective-permute-start | bytes 3145736 | tf_op jit(solution)/shard_map/ppermute | solution.py:44
  176.4 428.0 %reduce-scatter.7.cloned.1.call-start = ((), (), s32[]{:S(2)}) async-start(), calls=%async_computation.9 | async-start | bytes 1310720 | tf_op jit(solution)/shard_map/reduce_scatter | solution.py:438
  201.9 23.6 %collective-permute-start.28 = (bf16[256,2048]{1,0:T(8,128)(2,1)S(1)}, bf16[256,2048]{1,0:T(8,128)(2,1)S(1)}, u32[]{:S(2)}, u32[]{:S(2)}) collective-permute-start(bf16[256,2048]{1,0:T(8,128)(2,1)S(1)} %get-tuple-element.51), channel_id=1, source_target_pairs={{0,4},{1,5},{2,6},{3,7},{4,0},{5,1},{6,2},{7,3},{8,12},{9,13},{10,... | collective-permute-start | bytes 3145736 | tf_op jit(solution)/shard_map/ppermute | solution.py:44
  202.6 23.5 %collective-permute-start.27 = (bf16[256,2048]{1,0:T(8,128)(2,1)S(1)}, bf16[256,2048]{1,0:T(8,128)(2,1)S(1)}, u32[]{:S(2)}, u32[]{:S(2)}) collective-permute-start(bf16[256,2048]{1,0:T(8,128)(2,1)S(1)} %get-tuple-element.51), channel_id=1, source_target_pairs={{0,2},{1,3},{2,0},{3,1},{4,6},{5,7},{6,4},{7,5},{8,10},{9,11},{10,... | collective-permute-start | bytes 3145736 | tf_op jit(solution)/shard_map/ppermute | solution.py:44
  203.7 35.6 %collective-permute-start.31 = (bf16[256,2048]{1,0:T(8,128)(2,1)S(1)}, bf16[256,2048]{1,0:T(8,128)(2,1)S(1)}, u32[]{:S(2)}, u32[]{:S(2)}) collective-permute-start(bf16[256,2048]{1,0:T(8,128)(2,1)S(1)} %get-tuple-element.51), channel_id=1, source_target_pairs={{0,1},{1,0},{2,3},{3,2},{4,5},{5,4},{6,7},{7,6},{8,9},{9,8},{10,11... | collective-permute-start | bytes 3145736 | tf_op jit(solution)/shard_map/ppermute | solution.py:44
  293.3 23.8 %collective-permute-start.45 = (bf16[256,2048]{1,0:T(8,128)(2,1)S(1)}, bf16[256,2048]{1,0:T(8,128)(2,1)S(1)}, u32[]{:S(2)}, u32[]{:S(2)}) collective-permute-start(bf16[256,2048]{1,0:T(8,128)(2,1)S(1)} %convolution_convert_fusion.13), channel_id=1, source_target_pairs={{0,1},{1,0},{2,3},{3,2},{4,5},{5,4},{6,7},{7,6},{8,9},{9,8},{10,11... | collective-permute-start | bytes 3145736 | tf_op jit(solution)/shard_map/ppermute | solution.py:44
  344.1 33.9 %collective-permute-start.58 = (bf16[256,2048]{1,0:T(8,128)(2,1)S(1)}, bf16[256,2048]{1,0:T(8,128)(2,1)S(1)}, u32[]{:S(2)}, u32[]{:S(2)}) collective-permute-start(bf16[256,2048]{1,0:T(8,128)(2,1)S(1)} %get-tuple-element.47), channel_id=1, source_target_pairs={{0,1},{1,0},{2,3},{3,2},{4,5},{5,4},{6,7},{7,6},{8,9},{9,8},{10,11... | collective-permute-start | bytes 3145736 | tf_op jit(solution)/shard_map/ppermute | solution.py:44
  386.9 230.1 %reduce-scatter.11.cloned.1.call-start = ((), (), s32[]{:S(2)}) async-start(), calls=%async_computation.11 | async-start | bytes 5242880 | tf_op jit(solution)/shard_map/reduce_scatter | solution.py:444
  401.1 218.7 %reduce-scatter.9.cloned.1.call-start = ((), (), s32[]{:S(2)}) async-start(), calls=%async_computation.10 | async-start | bytes 5242880 | tf_op jit(solution)/shard_map/reduce_scatter | solution.py:441
  405.9 54.0 %collective-permute-start.36 = (bf16[256,2048]{1,0:T(8,128)(2,1)}, bf16[256,2048]{1,0:T(8,128)(2,1)}, u32[]{:S(2)}, u32[]{:S(2)}) collective-permute-start(bf16[256,2048]{1,0:T(8,128)(2,1)} %convolution_convert_fusion.17), channel_id=1, source_target_pairs={{0,1},{1,0},{2,3},{3,2},{4,5},{5,4},{6,7},{7,6},{8,9},{9,8},{10,11... | collective-permute-start | bytes 3145736 | tf_op jit(solution)/shard_map/ppermute | solution.py:44
  428.2 207.6 %reduce-scatter.5.cloned.1.call-start = ((), (), s32[]{:S(2)}) async-start(), calls=%async_computation.8 | async-start | bytes 3932160 | tf_op jit(solution)/shard_map/reduce_scatter | solution.py:435
  524.2 25.4 %collective-permute-start.76 = (bf16[256,2048]{1,0:T(8,128)(2,1)S(1)}, bf16[256,2048]{1,0:T(8,128)(2,1)}, u32[]{:S(2)}, u32[]{:S(2)}) collective-permute-start(bf16[256,2048]{1,0:T(8,128)(2,1)S(1)} %convolution_convert_fusion.24), channel_id=1, source_target_pairs={{0,1},{1,0},{2,3},{3,2},{4,5},{5,4},{6,7},{7,6},{8,9},{9,8},{10,11... | collective-permute-start | bytes 3145736 | tf_op jit(solution)/shard_map/ppermute | solution.py:44
  528.8 26.6 %collective-permute-start.74 = (bf16[512,2048]{1,0:T(8,128)(2,1)}, bf16[512,2048]{1,0:T(8,128)(2,1)}, u32[]{:S(2)}, u32[]{:S(2)}) collective-permute-start(bf16[512,2048]{1,0:T(8,128)(2,1)} %convolution_convert_fusion.9), channel_id=1, source_target_pairs={{0,1},{1,0},{2,3},{3,2},{4,5},{5,4},{6,7},{7,6},{8,9},{9,8},{10,11... | collective-permute-start | bytes 6291464 | tf_op jit(solution)/shard_map/ppermute | solution.py:44
  549.5 23.4 %collective-permute-start.73 = (bf16[256,2048]{1,0:T(8,128)(2,1)}, bf16[256,2048]{1,0:T(8,128)(2,1)}, u32[]{:S(2)}, u32[]{:S(2)}) collective-permute-start(bf16[256,2048]{1,0:T(8,128)(2,1)} %convolution_convert_fusion.26), channel_id=1, source_target_pairs={{0,1},{1,0},{2,3},{3,2},{4,5},{5,4},{6,7},{7,6},{8,9},{9,8},{10,11... | collective-permute-start | bytes 3145736 | tf_op jit(solution)/shard_map/ppermute | solution.py:44
  573.0 26.7 %collective-permute-start.93 = (f32[1536]{0:T(1024)S(1)}, f32[1536]{0:T(1024)S(1)}, u32[]{:S(2)}, u32[]{:S(2)}) collective-permute-start(f32[1536]{0:T(1024)S(1)} %pad_maximum_fusion.2), channel_id=1, source_target_pairs={{0,16},{8,24},{16,0},{24,8},{1,17},{9,25},{17,1},{25,9},{2,18},{10... | collective-permute-start | bytes 18440 | tf_op jit(solution)/shard_map/ppermute | solution.py:99
  (119 other events, 1672.6 us)
Sparse Core Ops, SparseCore 0:
  10.2 66.1 all-gather.4
  77.9 26.6 all-gather.6
  106.2 80.1 all-gather.8
  187.7 79.2 all-gather.10
  387.1 24.8 reduce-scatter.6
  414.1 77.3 reduce-scatter.10
  493.8 77.3 reduce-scatter.8
  573.5 62.2 reduce-scatter.4

commit v3 on v2

--- a/solution.py
+++ b/solution.py
@@ -19,8 +19,12 @@
     return centred * lax.rsqrt(variance + EPSILON) * gain_vec + bias_vec
 
 
-def gelu_tanh(values):
-    return jax.nn.gelu(values, approximate=True)
+def gelu_pair(values):
+    squared = values * values
+    bent = jnp.tanh(GELU_RATE * values * (1.0 + GELU_CUBE * squared))
+    upper = 0.5 * (1.0 + bent)
+    slope = upper + 0.5 * values * (1.0 - bent * bent) * GELU_RATE * (1.0 + 3.0 * GELU_CUBE * squared)
+    return values * upper, slope
 
 
 def contract_rows(left, right):
@@ -38,58 +42,100 @@
 SWAP_TP = 8
 BLOCK = 256
 LOG2_E = 1.4426950408889634
+GELU_RATE = 0.7978845608028654
+GELU_CUBE = 0.044715
 
 
 def exchange(piece, mask):
     return lax.ppermute(piece, "tp", [(at, at ^ mask) for at in range(SWAP_TP)])
 
 
-def gather_rows(piece):
+def tie(*values):
+    return lax.optimization_barrier(values)
+
+
+def gather_first(piece):
     if lax.axis_size("tp") != SWAP_TP:
-        return lax.all_gather(piece, "tp", axis=0, tiled=True)
+        return (lax.all_gather(piece, "tp", axis=0, tiled=True),)
+    return piece, exchange(piece, 2), exchange(piece, 4), exchange(piece, 1)
+
+
+def gather_second(state):
+    if len(state) == 1:
+        return state
+    piece, from_x, from_y, own_twin = state
     half = piece.shape[0] // 2
-    from_x = exchange(piece, 2)
-    from_y = exchange(piece, 4)
-    own_twin = exchange(piece, 1)
     far_low = exchange(from_x[:half], 4)
     far_high = exchange(from_y[half:], 2)
-    parts = [from_x, from_y, far_low, far_high]
-    twins = [exchange(part, 1) for part in parts]
-    return jnp.concatenate([piece, *parts, own_twin, *twins], axis=0)
+    return piece, from_x, from_y, far_low, far_high, own_twin, exchange(from_x, 1), exchange(from_y, 1)
+
+
+def gather_last(state):
+    if len(state) == 1:
+        return state[0]
+    far_low, far_high = state[3:5]
+    return jnp.concatenate([*state, exchange(far_low, 1), exchange(far_high, 1)], axis=0)
+
+
+def gather_rows(piece):
+    return gather_last(gather_second(gather_first(piece)))
 
 
 def add_low(left, right):
     return (left.astype(jnp.float32) + right.astype(jnp.float32)).astype(jnp.bfloat16)
 
 
-def scatter_rows(left, multiply):
-    tp_count = lax.axis_size("tp")
-    if tp_count != SWAP_TP:
-        return lax.psum_scatter(multiply(left), "tp", scatter_dimension=0, tiled=True).astype(
-            jnp.float32
-        )
+def scatter_multiply(left, multiply):
+    if lax.axis_size("tp") != SWAP_TP:
+        return (multiply(left),)
     rows = left.shape[0] // SWAP_TP
-    half = rows // 2
 
     def both(first, count):
         twin = multiply(left[(4 + first) * rows : (4 + first + count) * rows])
         return add_low(multiply(left[first * rows : (first + count) * rows]), exchange(twin, 1))
 
-    far = both(3, 1)
-    far_low = exchange(far[:half], 2)
-    far_high = exchange(far[half:], 4)
-    mixed = both(1, 2)
+    return both(3, 1), both(1, 2), both(0, 1)
+
+
+def scatter_first(parts):
+    if len(parts) == 1:
+        return (lax.psum_scatter(parts[0], "tp", scatter_dimension=0, tiled=True),)
+    far, mixed, home = parts
+    rows = far.shape[0]
+    half = rows // 2
     to_x, to_y = mixed[:rows], mixed[rows:]
-    x_low = exchange(to_x[:half], 2)
-    y_high = exchange(to_y[half:], 4)
-    home = both(0, 1)
-    x_high = exchange(add_low(to_x[half:], far_high), 2)
-    y_low = exchange(add_low(to_y[:half], far_low), 4)
-    wide = [part.astype(jnp.float32) for part in (x_low, x_high, y_low, y_high)]
     return (
-        home.astype(jnp.float32)
-        + jnp.concatenate(wide[:2], axis=0)
-        + jnp.concatenate(wide[2:], axis=0)
+        exchange(far[:half], 2),
+        exchange(far[half:], 4),
+        exchange(to_x[:half], 2),
+        exchange(to_y[half:], 4),
+        to_x[half:],
+        to_y[:half],
+        home,
+    )
+
+
+def scatter_second(state):
+    if len(state) == 1:
+        return state
+    far_low, far_high, x_low, y_high, to_x, to_y, home = state
+    return (
+        x_low,
+        exchange(add_low(to_x, far_high), 2),
+        exchange(add_low(to_y, far_low), 4),
+        y_high,
+        home,
+    )
+
+
+def scatter_last(state):
+    if len(state) == 1:
+        return state[0].astype(jnp.float32)
+    x_low, x_high, y_low, y_high, home = (part.astype(jnp.float32) for part in state)
+    return (
+        home
+        + jnp.concatenate([x_low, x_high], axis=0)
+        + jnp.concatenate([y_low, y_high], axis=0)
     )
 
 
@@ -357,113 +403,119 @@
     qkv_flat = qkv_full.reshape(width, 3 * head_cols)
     qkv_shift = jnp.concatenate([qv_bias[0], jnp.zeros_like(qv_bias[0]), qv_bias[1]])
     norm1_rows = gather_rows(norm1)
+    later_grad, norm1_rows = tie(out_grad, norm1_rows)
+    grad_state = gather_first(later_grad)
     qkv_rows = (
-        jnp.dot(
-            norm1_rows,
-            qkv_flat,
-            preferred_element_type=jnp.float32,
-        )
-        + qkv_shift
+        jnp.dot(norm1_rows, qkv_flat, preferred_element_type=jnp.float32) + qkv_shift
     ).astype(jnp.bfloat16)
-    out_grad, norm1_rows = lax.optimization_barrier((out_grad, norm1_rows))
-    grad_piece = gather_rows(out_grad)
+    grad_state, qkv_rows = tie(grad_state, qkv_rows)
+    grad_state = gather_second(grad_state)
     context, lse = attend(table, qkv_rows, head_cols)
-    context, grad_piece = lax.optimization_barrier((context, grad_piece))
-    attn_rows = scatter_rows(
+    grad_state, context = tie(grad_state, context)
+
+    attn_parts = scatter_multiply(
         context,
         lambda part: jnp.dot(part, out_full, preferred_element_type=jnp.float32).astype(
             jnp.bfloat16
         ),
     )
+    attn_rows = scatter_last(scatter_second(scatter_first(attn_parts)))
     middle = inputs + attn_rows + out_bias
     norm2 = layer_norm(middle, ln2_gain, ln2_bias).astype(jnp.bfloat16)
-    norm_piece = gather_rows(norm2)
-    pre = (
-        jnp.dot(
-            norm_piece,
-            up_full,
-            preferred_element_type=jnp.float32,
+    norm2_state = gather_first(norm2)
+    grad_state, norm2_state = tie(grad_state, norm2_state)
+    grad_piece = gather_last(grad_state)
+    norm_piece = gather_last(gather_second(norm2_state))
+    pre = jnp.dot(norm_piece, up_full, preferred_element_type=jnp.float32) + up_bias
+    act_value, slope = gelu_pair(pre)
+    act_rows, slope = tie(act_value.astype(jnp.bfloat16), slope.astype(jnp.bfloat16))
+
+    down_acc = contract_rows(act_rows, grad_piece).astype(jnp.bfloat16)
+    down_full, down_acc = tie(down_full, down_acc)
+    act_grad = contract_cols(grad_piece, down_full)
+    pre_grad = (act_grad * slope.astype(jnp.float32)).astype(jnp.bfloat16)
+    shift_acc = jnp.sum(pre_grad.astype(jnp.float32), axis=0)
+    norm2_grad_state = scatter_first(
+        scatter_multiply(
+            pre_grad, lambda part: contract_cols(part, up_full).astype(jnp.bfloat16)
         )
-        + up_bias
-    )
-    act_rows = gelu_tanh(pre).astype(jnp.bfloat16)
-    mlp_rows = scatter_rows(
+    )
+    up_acc = contract_rows(norm_piece, pre_grad).astype(jnp.bfloat16)
+    norm2_grad_state, up_acc = tie(norm2_grad_state, up_acc)
+    norm2_grad = scatter_last(scatter_second(norm2_grad_state))
+    unused_two, ln2_back = jax.vjp(layer_norm, middle, ln2_gain, ln2_bias)
+    middle_ln, grad_g2, grad_b2 = ln2_back(norm2_grad)
+    grad_rows = out_grad.astype(jnp.float32)
+    middle_grad = grad_rows + middle_ln
+    proj_grad, act_rows = tie(middle_grad.astype(jnp.bfloat16), act_rows)
+    portion_state = gather_first(proj_grad)
+    mlp_parts = scatter_multiply(
         act_rows,
         lambda part: jnp.dot(part, down_full, preferred_element_type=jnp.float32).astype(
             jnp.bfloat16
         ),
     )
+    portion_state, mlp_parts = tie(portion_state, mlp_parts)
+    portion = gather_last(gather_second(portion_state))
+    portion, mlp_parts = tie(portion, mlp_parts)
+    mlp_state = scatter_first(mlp_parts)
+    ctx_grad = contract_cols(portion, out_full).astype(jnp.bfloat16)
+    out_acc = contract_rows(context, portion).astype(jnp.bfloat16)
+    out_acc, ctx_grad = tie(out_acc, ctx_grad)
+    qkv_grad, qv_sums = attend_back(table, qkv_rows, context, ctx_grad, lse)
+    mlp_state, qkv_grad = tie(mlp_state, qkv_grad)
+    mlp_rows = scatter_last(scatter_second(mlp_state))
     layer_out = (middle + mlp_rows + down_bias).astype(jnp.bfloat16)
-    grad_rows = out_grad.astype(jnp.float32)
-    act_value, gelu_back = jax.vjp(gelu_tanh, pre)
-    act_piece = act_value.astype(jnp.bfloat16)
-    down_acc = contract_rows(act_piece, grad_piece)
-    act_grad = contract_cols(grad_piece, down_full)
-    pre_grad = gelu_back(act_grad)[0].astype(jnp.bfloat16)
-    up_acc = contract_rows(norm_piece, pre_grad)
-    shift_acc = jnp.sum(pre_grad.astype(jnp.float32), axis=0)
-    norm2_grad = scatter_rows(
-        pre_grad, lambda part: contract_cols(part, up_full).astype(jnp.bfloat16)
-    )
-    unused_two, ln2_back = jax.vjp(layer_norm, middle, ln2_gain, ln2_bias)
-    middle_ln, grad_g2, grad_b2 = ln2_back(norm2_grad)
-    middle_grad = grad_rows + middle_ln
-    proj_grad = middle_grad.astype(jnp.bfloat16)
-    portion = gather_rows(proj_grad)
-    out_acc = contract_rows(context, portion)
-    ctx_grad = contract_cols(portion, out_full).astype(jnp.bfloat16)
-    grad_out_w = out_acc
-    qkv_grad, sums = attend_back(table, qkv_rows, context, ctx_grad, lse)
-    early = sum_over(
-        sum_over(
-            jnp.stack([jnp.sum(middle_grad, axis=0), grad_g2, grad_b2, jnp.sum(grad_rows, axis=0)]),
-            "fsdp",
-        ),
-        "tp",
-    )
-    qkv_grad, early = lax.optimization_barrier((qkv_grad, early))
-    qv_sums = sums[:2]
-    norm1_grad = scatter_rows(
-        qkv_grad, lambda part: contract_cols(part, qkv_flat).astype(jnp.bfloat16)
-    )
+
+    norm1_grad_state = scatter_first(
+        scatter_multiply(
+            qkv_grad, lambda part: contract_cols(part, qkv_flat).astype(jnp.bfloat16)
+        )
+    )
+    grad_qkv_w = contract_rows(norm1_rows, qkv_grad).astype(jnp.bfloat16)
+    norm1_grad_state, grad_qkv_w = tie(norm1_grad_state, grad_qkv_w)
+    norm1_grad = scatter_last(scatter_second(norm1_grad_state))
     unused_one, ln1_back = jax.vjp(layer_norm, inputs, ln1_gain, ln1_bias)
     input_ln, grad_g1, grad_b1 = ln1_back(norm1_grad)
     tokens_grad = (middle_grad + input_ln).astype(jnp.bfloat16)
-    grad_qkv_flat = contract_rows(norm1_rows, qkv_grad)
-    grad_qkv_w = grad_qkv_flat.reshape(width, 3, head_cols)
-    shard_qkv, shard_out, shard_up, shard_down = (
-        lax.psum_scatter(
-            grad_qkv_w.astype(jnp.bfloat16), "fsdp", scatter_dimension=0, tiled=True
-        ).astype(jnp.float32),
-        lax.psum_scatter(
-            grad_out_w.astype(jnp.bfloat16), "fsdp", scatter_dimension=1, tiled=True
-        ).astype(jnp.float32),
-        lax.psum_scatter(
-            up_acc.astype(jnp.bfloat16), "fsdp", scatter_dimension=0, tiled=True
-        ).astype(jnp.float32),
-        lax.psum_scatter(
-            down_acc.astype(jnp.bfloat16), "fsdp", scatter_dimension=1, tiled=True
-        ).astype(jnp.float32),
-    )
-    own_sums = sum_over(jnp.concatenate([qv_sums.reshape(-1), shift_acc]), "fsdp")
-    grad_qv = own_sums[: 2 * head_cols].reshape(2, head_cols)
-    grad_upb_own = own_sums[2 * head_cols :]
-    late = sum_over(sum_over(jnp.stack([grad_g1, grad_b1]), "fsdp"), "tp")
+
+    def sum_weights(partial_sums, axis):
+        return lax.psum_scatter(
+            partial_sums, "fsdp", scatter_dimension=axis, tiled=True
+        ).astype(jnp.float32)
+
+    shard_down = sum_weights(down_acc, 1)
+    shard_up = sum_weights(up_acc, 0)
+    shard_out = sum_weights(out_acc, 1)
+    shard_qkv = sum_weights(grad_qkv_w.reshape(width, 3, head_cols), 0)
+    wide_sums = [
+        jnp.sum(middle_grad, axis=0),
+        grad_g2,
+        grad_b2,
+        jnp.sum(grad_rows, axis=0),
+        grad_g1,
+        grad_b1,
+    ]
+    summed = sum_over(
+        jnp.concatenate([*wide_sums, qv_sums[0], qv_sums[1], shift_acc]), "fsdp"
+    )
+    wide = sum_over(summed[: 6 * width], "tp").reshape(6, width)
+    own = summed[6 * width :]
     return (
         layer_out,
         tokens_grad,
-        late[0],
-        late[1],
+        wide[4],
+        wide[5],
         shard_qkv,
-        grad_qv,
+        own[: 2 * head_cols].reshape(2, head_cols),
         shard_out,
-        early[0],
-        early[1],
-        early[2],
+        wide[0],
+        wide[1],
+        wide[2],
         shard_up,
-        grad_upb_own,
+        own[2 * head_cols :],
         shard_down,
-        early[3],
+        wide[3],
     )
 
 

time: 655 us -> 623 us (0.951)
  waiting for transfers between devices: 263 us -> 243 us
  Pallas kernels: 54.5 us -> 35.7 us
  local copies, waits for them, and re-layouts: 51.2 us -> 68.6 us
  other arithmetic: 25.3 us -> 40.2 us
  matrix products: 160 us -> 147 us
  starting transfers between devices: 75.9 us -> 68.7 us
    ppermute x72, waiting for transfers between devices: 237 us -> 156 us  [exchange(): return lax.ppermute(piece, 'tp', [(at, at ^ mask) for at in range(SWAP_TP)])]
    all_gather x1, waiting for transfers between devices: 8.21 us -> 37.5 us  [gather_weights(): lax.all_gather(down_weight, 'fsdp', axis=1, tiled=True)]
    reduce_scatter x4, waiting for transfers between devices: 13.2 us -> 34.3 us  [sum_weights(): lax.psum_scatter(partial_sums, 'fsdp', scatter_dimension=axis, tiled=True)]
    dot_general x6, matrix products: 25.6 us -> 13.1 us  [local(): jnp.dot(part, down_full, preferred_element_type=jnp.float32)]
    all_gather x1, waiting for transfers between devices: 0.01 us -> 11.8 us  [gather_weights(): lax.all_gather(qkv_weight, 'fsdp', axis=0, tiled=True)]
    pallas_call x1, Pallas kernels: 28.6 us -> 18.9 us  [attend_back(): pl.pallas_call(attend_back_kernel, out_shape=(jax.ShapeDtypeStruct(qkv_ro...]
    unnamed x116 -> x159, local copies, waits for them, and re-layouts: 37.4 us -> 47 us
    pallas_call x1, Pallas kernels: 25.9 us -> 16.8 us  [attend(): pl.pallas_call(attend_kernel, out_shape=(jax.ShapeDtypeStruct((rows, head...]
  transfers between devices with their start and end apart: 103 -> 90, of which waited for: 45 -> 37; matrix products, arithmetic and copies ran while one was open for 30% -> 34% of each run, Pallas kernels for 8% -> 6%
where the time goes in v3:
time: 623 us; the launch traced here: 620 us
  waiting for transfers between devices  243 us (39%)
  matrix products  147 us (24%)
  starting transfers between devices  68.7 us (11%)
  local copies, waits for them, and re-layouts  68.6 us (11%)
  other arithmetic  40.2 us (6%)
  Pallas kernels  35.7 us (6%)
  between operations  15.6 us (3%)
    ppermute x72, waiting for transfers between devices, exchange(): return lax.ppermute(piece, 'tp', [(at, at ^ mask) for at in range(SWAP_TP)])  156 us
    dot_general x14, matrix products, contract_cols(): lax.dot_general(left, right, (((1,), (1,)), ((), ())), preferred_element_...  56.6 us
    ppermute x72, starting transfers between devices, exchange(): return lax.ppermute(piece, 'tp', [(at, at ^ mask) for at in range(SWAP_TP)])  53 us
    unnamed x159, local copies, waits for them, and re-layouts  47 us
    all_gather x1, waiting for transfers between devices, gather_weights(): lax.all_gather(down_weight, 'fsdp', axis=1, tiled=True)  37.5 us
    dot_general x4, matrix products, contract_rows(): lax.dot_general(left, right, (((0,), (0,)), ((), ())), preferred_element_...  35.8 us
    reduce_scatter x4, waiting for transfers between devices, sum_weights(): lax.psum_scatter(partial_sums, 'fsdp', scatter_dimension=axis, tiled=True)  34.3 us
    pallas_call x1, Pallas kernels, attend_back(): pl.pallas_call(attend_back_kernel, out_shape=(jax.ShapeDtypeStruct(qkv_ro...  18.9 us
  transfers between devices with their start and end apart: 90, of which 37 were waited for; matrix products, arithmetic and copies ran while one was open for 34% of the time, Pallas kernels for 6%

profile of v3, /device:TPU:0, one launch (start us, length us, event | category | flops | bytes accessed | tf_op | source)
XLA Modules:
  0.0 619.8 jit_solution(7646057255610294597)
XLA Ops:
  18.1 21.7 %collective-permute-done.1 = bf16[256,2048]{1,0:T(8,128)(2,1)S(1)} collective-permute-done((bf16[256,2048]{1,0:T(8,128)(2,1)}, bf16[256,2048]{1,0:T(8,128)(2,1)S(1)}, u32[]{:S(2)}, u32[]{:S(2)}) %collective-permute-start.1) | collective-permute-done | bytes 1048608 | tf_op jit(solution)/shard_map/ppermute | solution.py:50
  64.6 11.8 %all-gather.5.cloned.1.call-done = bf16[2048,3,256]{0,2,1:T(8,128)(2,1)} async-done(((bf16[512,3,256]{0,2,1:T(8,128)(2,1)}), bf16[2048,3,256]{0,2,1:T(8,128)(2,1)}) %all-gather.5.cloned.1.call-update) | async-done | bytes 3145744 | tf_op jit(solution)/shard_map/all_gather | solution.py:394
  76.4 11.3 %add_convert_fusion.1.qkv = bf16[2048,768]{1,0:T(8,128)(2,1)} fusion(f32[768]{0:T(1024)S(1)} %pad_maximum_fusion, bf16[2048,2048]{1,0:T(8,128)(2,1)} %constant_dynamic-update-slice_fusion, bf16[2048,768]{0,1:T(8,128)(2,1)} %bitcast.58), kind=kOutput, calls=%fused_computation.6 | convolution fusion | flops 6445596672 | bytes 14683136 | tf_op jit(solution)/shard_map/dot_general | solution.py:409
  94.9 16.8 %attend.1 = (bf16[2048,256]{1,0:T(8,128)(2,1)}, f32[16,2048]{1,0:T(8,128)}) custom-call(s32[3,8]{1,0:T(4,128)} %pad_add_fusion.table, bf16[2048,768]{1,0:T(8,128)(2,1)} %add_convert_fusion.1.qkv), custom_call_target="tpu_custom_call" | custom-call | tf_op jit(solution)/shard_map/attend/pallas_call | solution.py:335
  126.8 8.7 %collective-permute-done.22 = bf16[128,2048]{1,0:T(8,128)(2,1)S(1)} collective-permute-done((bf16[128,2048]{1,0:T(8,128)(2,1)S(1)}, bf16[128,2048]{1,0:T(8,128)(2,1)S(1)}, u32[]{:S(2)}, u32[]{:S(2)}) %collective-permute-start.22) | collective-permute-done | bytes 524320 | tf_op jit(solution)/shard_map/ppermute | solution.py:50
  140.7 10.6 %collective-permute-done.23 = bf16[128,2048]{1,0:T(8,128)(2,1)S(1)} collective-permute-done((bf16[128,2048]{1,0:T(8,128)(2,1)S(1)}, bf16[128,2048]{1,0:T(8,128)(2,1)S(1)}, u32[]{:S(2)}, u32[]{:S(2)}) %collective-permute-start.23) | collective-permute-done | bytes 524320 | tf_op jit(solution)/shard_map/ppermute | solution.py:50
  152.7 7.6 %collective-permute-done.24 = bf16[128,2048]{1,0:T(8,128)(2,1)S(1)} collective-permute-done((bf16[128,2048]{1,0:T(8,128)(2,1)S(1)}, bf16[128,2048]{1,0:T(8,128)(2,1)S(1)}, u32[]{:S(2)}, u32[]{:S(2)}) %collective-permute-start.24) | collective-permute-done | bytes 524320 | tf_op jit(solution)/shard_map/ppermute | solution.py:50
  168.4 22.9 %collective-permute-done.26 = bf16[256,2048]{1,0:T(8,128)(2,1)} collective-permute-done((bf16[256,2048]{1,0:T(8,128)(2,1)}, bf16[256,2048]{1,0:T(8,128)(2,1)}, u32[]{:S(2)}, u32[]{:S(2)}) %collective-permute-start.26) | collective-permute-done | bytes 1048608 | tf_op jit(solution)/shard_map/ppermute | solution.py:50
  219.8 18.1 %add_convert_fusion = (bf16[2048,1024]{1,0:T(8,128)(2,1)}, bf16[2048,1024]{1,0:T(8,128)(2,1)S(1)}) fusion(f32[1024]{0:T(1024)S(1)} %copy-done.51, bf16[2048,2048]{1,0:T(8,128)(2,1)} %constant_dynamic-update-slice_fusion.20, bf16[2048,1024]{1,0:T(8,128)(2,1)} %all-gather.11.cloned.1.call-done), kind=kOutput, calls=%fused_computation.2 | convolution fusion | flops 8631877632 | bytes 20975616 | tf_op jit(solution)/shard_map/dot_general | solution.py:429
  240.0 11.1 %convolution_convert_fusion = bf16[1024,2048]{1,0:T(8,128)(2,1)} fusion(bf16[2048,1024]{1,0:T(8,128)(2,1)S(1)} %get-tuple-element.129, bf16[2048,2048]{1,0:T(8,128)(2,1)S(1)} %copy-done.32), kind=kOutput, calls=%fused_computation.11 | convolution fusion | flops 8592031744 | bytes 16777216 | tf_op jit(solution)/shard_map/dot_general | solution.py:31
  251.1 37.5 %all-gather.9.cloned.1.call-done = bf16[1024,2048]{1,0:T(8,128)(2,1)} async-done(((bf16[1024,512]{1,0:T(8,128)(2,1)}), bf16[1024,2048]{1,0:T(8,128)(2,1)}) %all-gather.9.cloned.1.call-update) | async-done | bytes 4194320 | tf_op jit(solution)/shard_map/all_gather | solution.py:397
  288.6 25.2 %convert_reduce_fusion = (f32[1024]{0:T(1024)S(1)}, bf16[2048,1024]{1,0:T(8,128)(2,1)S(1)}) fusion(bf16[2048,1024]{1,0:T(8,128)(2,1)} %get-tuple-element.120, bf16[2048,2048]{1,0:T(8,128)(2,1)} %copy-done.31, bf16[1024,2048]{1,0:T(8,128)(2,1)} %all-gather.9.cloned.1.call-done), kind=kOutput, calls=%fused_computation | convolution fusion | flops 8600419328 | bytes 20975616 | tf_op jit(solution)/shard_map/dot_general | solution.py:37
  332.3 12.7 %convolution_convert_fusion.1 = bf16[2048,1024]{1,0:T(8,128)(2,1)} fusion(bf16[2048,2048]{1,0:T(8,128)(2,1)} %constant_dynamic-update-slice_fusion.20, bf16[2048,1024]{1,0:T(8,128)(2,1)S(1)} %get-tuple-element.248), kind=kOutput, calls=%fused_computation.12 | convolution fusion | flops 8592031744 | bytes 16777216 | tf_op jit(solution)/shard_map/dot_general | solution.py:31
  357.6 8.7 %collective-permute-done.44 = bf16[128,2048]{1,0:T(8,128)(2,1)} collective-permute-done((bf16[128,2048]{1,0:T(8,128)(2,1)}, bf16[128,2048]{1,0:T(8,128)(2,1)}, u32[]{:S(2)}, u32[]{:S(2)}) %collective-permute-start.44) | collective-permute-done | bytes 524320 | tf_op jit(solution)/shard_map/ppermute | solution.py:50
  394.9 13.5 %collective-permute-done.46 = bf16[256,2048]{1,0:T(8,128)(2,1)S(1)} collective-permute-done((bf16[256,2048]{1,0:T(8,128)(2,1)S(1)}, bf16[256,2048]{1,0:T(8,128)(2,1)S(1)}, u32[]{:S(2)}, u32[]{:S(2)}) %collective-permute-start.46) | collective-permute-done | bytes 1048608 | tf_op jit(solution)/shard_map/ppermute | solution.py:50
  414.4 11.8 %collective-permute-done.51 = bf16[128,2048]{1,0:T(8,128)(2,1)S(1)} collective-permute-done((bf16[128,2048]{1,0:T(8,128)(2,1)S(1)}, bf16[128,2048]{1,0:T(8,128)(2,1)S(1)}, u32[]{:S(2)}, u32[]{:S(2)}) %collective-permute-start.51) | collective-permute-done | bytes 524320 | tf_op jit(solution)/shard_map/ppermute | solution.py:50
  435.8 6.8 %convolution_convert_fusion.27.ctx_grad = bf16[2048,256]{1,0:T(8,128)(2,1)} fusion(bf16[2048,2048]{1,0:T(8,128)(2,1)} %copy-done.5, bf16[256,2048]{1,0:T(8,128)(2,1)S(1)} %copy-done.4), kind=kOutput, calls=%fused_computation.69 | convolution fusion | flops 2148007936 | bytes 10485760 | tf_op jit(solution)/shard_map/dot_general | solution.py:37
  450.3 18.9 %attend_back.1 = (bf16[2048,768]{1,0:T(8,128)(2,1)}, f32[8,256]{1,0:T(8,128)}) custom-call(s32[3,8]{1,0:T(4,128)} %pad_add_fusion.table, bf16[2048,768]{1,0:T(8,128)(2,1)} %add_convert_fusion.1.qkv, bf16[2048,256]{1,0:T(8,128)(2,1)} %get-tuple-element.97.ctx, bf16[2048,256]{1,0:T(8,128)(2,1)} %convolution_convert_fusion.27.ctx_grad, ...), custom_call_target="tpu_custom_call" | custom-call | tf_op jit(solution)/shard_map/attend_back/pallas_call | solution.py:349
  489.6 8.5 %convolution_convert_fusion.2 = bf16[2048,768]{1,0:T(8,128)(2,1)} fusion(bf16[2048,2048]{1,0:T(8,128)(2,1)S(1)} %bitcast.52, bf16[2048,768]{1,0:T(8,128)(2,1)S(1)} %copy-done.49), kind=kOutput, calls=%fused_computation.13 | convolution fusion | flops 6444023808 | bytes 14680064 | tf_op jit(solution)/shard_map/dot_general | solution.py:31
  499.2 8.7 %collective-permute-done.68 = bf16[128,2048]{1,0:T(8,128)(2,1)} collective-permute-done((bf16[128,2048]{1,0:T(8,128)(2,1)S(1)}, bf16[128,2048]{1,0:T(8,128)(2,1)}, u32[]{:S(2)}, u32[]{:S(2)}) %collective-permute-start.68) | collective-permute-done | bytes 524320 | tf_op jit(solution)/shard_map/ppermute | solution.py:50
  520.7 8.8 %collective-permute-done.71 = bf16[128,2048]{1,0:T(8,128)(2,1)S(1)} collective-permute-done((bf16[128,2048]{1,0:T(8,128)(2,1)S(1)}, bf16[128,2048]{1,0:T(8,128)(2,1)S(1)}, u32[]{:S(2)}, u32[]{:S(2)}) %collective-permute-start.71) | collective-permute-done | bytes 524320 | tf_op jit(solution)/shard_map/ppermute | solution.py:50
  541.2 6.8 %collective-permute-start.73 = (f32[13824]{0:T(1024)S(1)}, f32[13824]{0:T(1024)S(1)}, u32[]{:S(2)}, u32[]{:S(2)}) collective-permute-start(f32[13824]{0:T(1024)S(1)} %constant_dynamic-update-slice_fusion.41), channel_id=1, source_target_pairs={{0,16},{8,24},{16,0},{24,8},{1,17},{9,25},{17,1},{25,9},{2,18},{10... | collective-permute-start | bytes 165896 | tf_op jit(solution)/shard_map/ppermute | solution.py:145
  556.4 5.5 collective-permute-done.61
  575.9 34.3 %reduce-scatter.5.cloned.1.call-done = bf16[512,3,256]{0,2,1:T(8,128)(2,1)} async-done(((bf16[2048,3,256]{0,2,1:T(8,128)(2,1)}), bf16[512,3,256]{0,2,1:T(8,128)(2,1)}) %reduce-scatter.5.cloned.1.call-update) | async-done | bytes 786448 | tf_op jit(solution)/shard_map/reduce_scatter | solution.py:483
  (427 shorter events, 255.9 us)
Async XLA Ops:
  7.2 69.1 %all-gather.5.cloned.1.call-start = ((), (), s32[]{:S(2)}) async-start(), calls=%async_computation.4 | async-start | bytes 3932160 | tf_op jit(solution)/shard_map/all_gather | solution.py:394
  9.7 103.1 %all-gather.7.cloned.1.call-start = ((), (), s32[]{:S(2)}) async-start(), calls=%async_computation.5 | async-start | bytes 1310720 | tf_op jit(solution)/shard_map/all_gather | solution.py:395
  13.4 26.4 %collective-permute-start.1 = (bf16[256,2048]{1,0:T(8,128)(2,1)}, bf16[256,2048]{1,0:T(8,128)(2,1)S(1)}, u32[]{:S(2)}, u32[]{:S(2)}) collective-permute-start(bf16[256,2048]{1,0:T(8,128)(2,1)} %get-tuple-element.207), channel_id=1, source_target_pairs={{0,4},{1,5},{2,6},{3,7},{4,0},{5,1},{6,2},{7,3},{8,12},{9,13},{10,... | collective-permute-start | bytes 3145736 | tf_op jit(solution)/shard_map/ppermute | solution.py:50
  16.4 25.2 %collective-permute-start = (bf16[256,2048]{1,0:T(8,128)(2,1)}, bf16[256,2048]{1,0:T(8,128)(2,1)}, u32[]{:S(2)}, u32[]{:S(2)}) collective-permute-start(bf16[256,2048]{1,0:T(8,128)(2,1)} %get-tuple-element.207), channel_id=1, source_target_pairs={{0,2},{1,3},{2,0},{3,1},{4,6},{5,7},{6,4},{7,5},{8,10},{9,11},{10,... | collective-permute-start | bytes 3145736 | tf_op jit(solution)/shard_map/ppermute | solution.py:50
  18.0 39.1 %collective-permute-start.4 = (bf16[256,2048]{1,0:T(8,128)(2,1)}, bf16[256,2048]{1,0:T(8,128)(2,1)S(1)}, u32[]{:S(2)}, u32[]{:S(2)}) collective-permute-start(bf16[256,2048]{1,0:T(8,128)(2,1)} %get-tuple-element.207), channel_id=1, source_target_pairs={{0,1},{1,0},{2,3},{3,2},{4,5},{5,4},{6,7},{7,6},{8,9},{9,8},{10,11... | collective-permute-start | bytes 3145736 | tf_op jit(solution)/shard_map/ppermute | solution.py:50
  18.0 201.8 %all-gather.11.cloned.1.call-start = ((), (), s32[]{:S(2)}) async-start(), calls=%async_computation.7 | async-start | bytes 5242880 | tf_op jit(solution)/shard_map/all_gather | solution.py:396
  62.0 25.6 %collective-permute-start.11 = (bf16[256,2048]{1,0:T(8,128)(2,1)S(1)}, bf16[256,2048]{1,0:T(8,128)(2,1)}, u32[]{:S(2)}, u32[]{:S(2)}) collective-permute-start(bf16[256,2048]{1,0:T(8,128)(2,1)S(1)} %copy-done.10), channel_id=1, source_target_pairs={{0,1},{1,0},{2,3},{3,2},{4,5},{5,4},{6,7},{7,6},{8,9},{9,8},{10,11... | collective-permute-start | bytes 3145736 | tf_op jit(solution)/shard_map/ppermute | solution.py:50
  62.5 25.1 %collective-permute-start.10 = (bf16[256,2048]{1,0:T(8,128)(2,1)S(1)}, bf16[256,2048]{1,0:T(8,128)(2,1)S(1)}, u32[]{:S(2)}, u32[]{:S(2)}) collective-permute-start(bf16[256,2048]{1,0:T(8,128)(2,1)S(1)} %copy-done.10), channel_id=1, source_target_pairs={{0,4},{1,5},{2,6},{3,7},{4,0},{5,1},{6,2},{7,3},{8,12},{9,13},{10,... | collective-permute-start | bytes 3145736 | tf_op jit(solution)/shard_map/ppermute | solution.py:50
  64.0 24.9 %collective-permute-start.9 = (bf16[256,2048]{1,0:T(8,128)(2,1)S(1)}, bf16[256,2048]{1,0:T(8,128)(2,1)}, u32[]{:S(2)}, u32[]{:S(2)}) collective-permute-start(bf16[256,2048]{1,0:T(8,128)(2,1)S(1)} %copy-done.10), channel_id=1, source_target_pairs={{0,2},{1,3},{2,0},{3,1},{4,6},{5,7},{6,4},{7,5},{8,10},{9,11},{10,... | collective-permute-start | bytes 3145736 | tf_op jit(solution)/shard_map/ppermute | solution.py:50
  119.5 169.2 %all-gather.9.cloned.1.call-start = ((), (), s32[]{:S(2)}) async-start(), calls=%async_computation.6 | async-start | bytes 5242880 | tf_op jit(solution)/shard_map/all_gather | solution.py:397
  165.4 25.9 %collective-permute-start.26 = (bf16[256,2048]{1,0:T(8,128)(2,1)}, bf16[256,2048]{1,0:T(8,128)(2,1)}, u32[]{:S(2)}, u32[]{:S(2)}) collective-permute-start(bf16[256,2048]{1,0:T(8,128)(2,1)} %add_convert_fusion.12), channel_id=1, source_target_pairs={{0,4},{1,5},{2,6},{3,7},{4,0},{5,1},{6,2},{7,3},{8,12},{9,13},{10,... | collective-permute-start | bytes 3145736 | tf_op jit(solution)/shard_map/ppermute | solution.py:50
  165.9 25.6 %collective-permute-start.25 = (bf16[256,2048]{1,0:T(8,128)(2,1)}, bf16[256,2048]{1,0:T(8,128)(2,1)}, u32[]{:S(2)}, u32[]{:S(2)}) collective-permute-start(bf16[256,2048]{1,0:T(8,128)(2,1)} %add_convert_fusion.12), channel_id=1, source_target_pairs={{0,2},{1,3},{2,0},{3,1},{4,6},{5,7},{6,4},{7,5},{8,10},{9,11},{10,... | collective-permute-start | bytes 3145736 | tf_op jit(solution)/shard_map/ppermute | solution.py:50
  167.2 399.4 %reduce-scatter.11.cloned.1.call-start = ((), (), s32[]{:S(2)}) async-start(), calls=%async_computation.11 | async-start | bytes 5242880 | tf_op jit(solution)/shard_map/reduce_scatter | solution.py:483
  320.4 24.5 %collective-permute-start.42 = (bf16[256,2048]{1,0:T(8,128)(2,1)}, bf16[256,2048]{1,0:T(8,128)(2,1)}, u32[]{:S(2)}, u32[]{:S(2)}) collective-permute-start(bf16[256,2048]{1,0:T(8,128)(2,1)} %convolution_convert_fusion.15), channel_id=1, source_target_pairs={{0,1},{1,0},{2,3},{3,2},{4,5},{5,4},{6,7},{7,6},{8,9},{9,8},{10,11... | collective-permute-start | bytes 3145736 | tf_op jit(solution)/shard_map/ppermute | solution.py:50
  324.5 25.5 %collective-permute-start.38 = (bf16[128,2048]{1,0:T(8,128)(2,1)}, bf16[128,2048]{1,0:T(8,128)(2,1)}, u32[]{:S(2)}, u32[]{:S(2)}) collective-permute-start(bf16[128,2048]{1,0:T(8,128)(2,1)} %get-tuple-element.231), channel_id=1, source_target_pairs={{0,4},{1,5},{2,6},{3,7},{4,0},{5,1},{6,2},{7,3},{8,12},{9,13},{10,... | collective-permute-start | bytes 1572872 | tf_op jit(solution)/shard_map/ppermute | solution.py:50
  325.9 24.0 %collective-permute-start.37 = (bf16[128,2048]{1,0:T(8,128)(2,1)}, bf16[128,2048]{1,0:T(8,128)(2,1)}, u32[]{:S(2)}, u32[]{:S(2)}) collective-permute-start(bf16[128,2048]{1,0:T(8,128)(2,1)} %get-tuple-element.232), channel_id=1, source_target_pairs={{0,2},{1,3},{2,0},{3,1},{4,6},{5,7},{6,4},{7,5},{8,10},{9,11},{10,... | collective-permute-start | bytes 1572872 | tf_op jit(solution)/shard_map/ppermute | solution.py:50
  357.1 212.3 %reduce-scatter.7.cloned.1.call-start = ((), (), s32[]{:S(2)}) async-start(), calls=%async_computation.9 | async-start | bytes 1310720 | tf_op jit(solution)/shard_map/reduce_scatter | solution.py:483
  383.2 25.1 %collective-permute-start.46 = (bf16[256,2048]{1,0:T(8,128)(2,1)S(1)}, bf16[256,2048]{1,0:T(8,128)(2,1)S(1)}, u32[]{:S(2)}, u32[]{:S(2)}) collective-permute-start(bf16[256,2048]{1,0:T(8,128)(2,1)S(1)} %fusion.70), channel_id=1, source_target_pairs={{0,4},{1,5},{2,6},{3,7},{4,0},{5,1},{6,2},{7,3},{8,12},{9,13},{10,... | collective-permute-start | bytes 3145736 | tf_op jit(solution)/shard_map/ppermute | solution.py:50
  385.2 25.2 %collective-permute-start.45 = (bf16[256,2048]{1,0:T(8,128)(2,1)S(1)}, bf16[256,2048]{1,0:T(8,128)(2,1)S(1)}, u32[]{:S(2)}, u32[]{:S(2)}) collective-permute-start(bf16[256,2048]{1,0:T(8,128)(2,1)S(1)} %fusion.70), channel_id=1, source_target_pairs={{0,2},{1,3},{2,0},{3,1},{4,6},{5,7},{6,4},{7,5},{8,10},{9,11},{10,... | collective-permute-start | bytes 3145736 | tf_op jit(solution)/shard_map/ppermute | solution.py:50
  442.6 130.5 %reduce-scatter.9.cloned.1.call-start = ((), (), s32[]{:S(2)}) async-start(), calls=%async_computation.10 | async-start | bytes 5242880 | tf_op jit(solution)/shard_map/reduce_scatter | solution.py:483
  443.4 166.8 %reduce-scatter.5.cloned.1.call-start = ((), (), s32[]{:S(2)}) async-start(), calls=%async_computation.8 | async-start | bytes 3932160 | tf_op jit(solution)/shard_map/reduce_scatter | solution.py:483
  444.9 24.3 %collective-permute-start.58 = (bf16[128,2048]{1,0:T(8,128)(2,1)}, bf16[128,2048]{1,0:T(8,128)(2,1)}, u32[]{:S(2)}, u32[]{:S(2)}) collective-permute-start(bf16[128,2048]{1,0:T(8,128)(2,1)} %get-tuple-element.229), channel_id=1, source_target_pairs={{0,4},{1,5},{2,6},{3,7},{4,0},{5,1},{6,2},{7,3},{8,12},{9,13},{10,... | collective-permute-start | bytes 1572872 | tf_op jit(solution)/shard_map/ppermute | solution.py:50
  446.3 22.9 %collective-permute-start.57 = (bf16[128,2048]{1,0:T(8,128)(2,1)}, bf16[128,2048]{1,0:T(8,128)(2,1)}, u32[]{:S(2)}, u32[]{:S(2)}) collective-permute-start(bf16[128,2048]{1,0:T(8,128)(2,1)} %get-tuple-element.230), channel_id=1, source_target_pairs={{0,2},{1,3},{2,0},{3,1},{4,6},{5,7},{6,4},{7,5},{8,10},{9,11},{10,... | collective-permute-start | bytes 1572872 | tf_op jit(solution)/shard_map/ppermute | solution.py:50
  520.1 34.4 %collective-permute-start.62 = (bf16[128,2048]{1,0:T(8,128)(2,1)S(1)}, bf16[128,2048]{1,0:T(8,128)(2,1)S(1)}, u32[]{:S(2)}, u32[]{:S(2)}) collective-permute-start(bf16[128,2048]{1,0:T(8,128)(2,1)S(1)} %add_convert_fusion.15), channel_id=1, source_target_pairs={{0,4},{1,5},{2,6},{3,7},{4,0},{5,1},{6,2},{7,3},{8,12},{9,13},{10,... | collective-permute-start | bytes 1572872 | tf_op jit(solution)/shard_map/ppermute | solution.py:50
  (123 other events, 1554.9 us)
Sparse Core Ops, SparseCore 0:
  10.2 66.1 all-gather.4
  77.9 26.6 all-gather.6
  119.6 88.3 all-gather.10
  209.4 79.2 all-gather.8
  357.3 74.3 reduce-scatter.10
  442.7 24.7 reduce-scatter.6
  469.9 75.8 reduce-scatter.8
  548.1 62.0 reduce-scatter.4
